TPU v7x, 256 devices: a whole 4x4x8 slice. The times are simulated.
256 devices in a mesh: cells: 32 (over x_lo, z, core), orb: 8 (over x_hi, y).
Axes of the slice: x: 4 (x_hi: 2, x_lo: 2; x = x_hi * 2 + x_lo), y: 4, z: 8, core: 2. Of those that a mesh axis runs over, the one named last changes fastest.
Arguments:
- orbitals: float32 [69312, 1024], P('cells', 'orb'), may hold values from -6 to 6
- occupations: float32 [1024], P('orb'), may hold values from 0.4 to 2.5
- external: float32 [69312], P('cells'), may hold values from -3 to 3
- core_density: float32 [69312], P('cells'), may hold values from 1 to 300
- cell_scale: float32 [288], P('cells'), may hold values from 0.5 to 2
- stiffness: float32 [343, 343], replicated, may hold values from -1 to 7, as said below
- touched_atom: int32 [192], replicated, may hold values from 0 to 63, as said below
- touched_cells: int32 [192, 1], P('cells'), may hold values from 0 to 8
- projectors: float32 [192, 1, 18, 343], P('cells'), may hold values from -1.2 to 1.2
- coupling: float32 [64, 18, 18], replicated, may hold values from -3 to 3, as said below
- atom_owner: int32 [64, 1], replicated, may hold values from 0 to 31; in each aligned block of 64 rows (0 to 63, 64 to 127, ...) at most 5 rows name the same one
Outputs:
- final_orbitals: float32 [69312, 1024], P('cells', 'orb')
- rayleigh: float32 [1024], P('orb')
- owned_projections: float32 [160, 18, 1024], P('cells', None, 'orb')
Inputs may be any that keep to these rules, and one draw needn't show every extreme that they name: `stiffness`: symmetric. `coupling`: each atom's matrix is symmetric. `touched_atom`: the 6 atoms of one device are distinct, and atom a's home index of cells, a // 2, lies within 2 of the device along the periodic cells axis. `touched_cells`: the cells in one row are distinct. `atom_owner`: no owner has more than 5 atoms, and some owner has exactly 5.
All inputs are finite; a program needn't handle non-finite values.
Results may differ from a plain program's by a relative error of at most 0.00011.
Values sent between devices are 32-bit elements; how exact they have to be, the bound alone decides.
A program may use at most 128 MiB of HBM per device.

v0:
```python
import math

import jax
import jax.numpy as jnp
from jax import lax
from jax.sharding import Mesh
from jax.sharding import PartitionSpec as P

DEG = 6
EDGE = 7
CELL_NODES = 343
SIDE = 3
THICK = 1
CELL_DEV = 9
ORB = 1024
TOUCH_DEV = 6
OWN_CAP = 5
CELLS = ("cells_0", "cells_1", "cells_2")


highest = lax.Precision.HIGHEST
step_size = 0.1
exchange_coef = (3.0 / math.pi) ** (1.0 / 3.0)
tiny = 1e-06


def from_everyone(value, axis):
    length = lax.axis_size(axis)
    return lax.all_to_all(
        jnp.broadcast_to(value[None], (length, *value.shape)), axis, 0, 0, tiled=True
    )


def over_copies(value, axis):
    return from_everyone(value, axis).sum(axis=0)


def passed_along(value, axis, steps):
    count = lax.axis_size(axis)
    pairs = [(source, (source + steps) % count) for source in range(count)]
    return lax.ppermute(value, axis, pairs)


def in_order(parts, dim):
    lengths = list(parts.shape[1:])
    lengths[dim] *= parts.shape[0]
    return jnp.moveaxis(parts, 0, dim).reshape(lengths)


def gather_axes(value, axes, dim):
    far, near = axes
    parts = from_everyone(from_everyone(value, far), near)
    return in_order(parts.swapaxes(0, 1).reshape(-1, *value.shape), dim)


def packed_total(arrays, axis):
    ends = [0]
    for a in arrays:
        ends.append(ends[-1] + a.size)
    so_far = over_copies(jnp.concatenate([a.ravel() for a in arrays]), axis)
    return tuple((so_far[b:e].reshape(a.shape) for a, b, e in zip(arrays, ends, ends[1:])))


def padded_to(lines, length):
    spare = -len(lines) % length
    return jnp.pad(lines, [(0, spare)] + [(0, 0)] * (lines.ndim - 1))


def collect(value, axis, dim):
    parts = from_everyone(value, axis)
    return in_order(parts, dim)


def cut_along(value, dim, length):
    before, after = (value.shape[:dim], value.shape[dim + 1 :])
    return jnp.moveaxis(value.reshape(*before, length, -1, *after), dim, 0)


def summed_on_arrival(value, axis, dim):
    parts = cut_along(value, dim, lax.axis_size(axis))
    arrived = lax.all_to_all(parts, axis, split_axis=0, concat_axis=0, tiled=True)
    return arrived.sum(axis=0)


def nested_sum(value, axes):
    lines = value.reshape(-1, value.shape[-1])
    padded = padded_to(lines, lax.axis_size(axes))
    whole = collect(summed_on_arrival(padded, axes, 0), axes, 0)
    return lax.slice_in_dim(whole, 0, len(lines)).reshape(value.shape)


def cut_cells(grid, upper_layer):
    layers = grid.shape[0]
    extended = jnp.concatenate([grid, upper_layer[None]], axis=0)
    slabs = jnp.stack([extended[offset : offset + layers : DEG] for offset in range(EDGE)], axis=1)
    blocks = [
        slabs[:, :, DEG * row_cell : DEG * row_cell + EDGE, DEG * col_cell : DEG * col_cell + EDGE]
        for row_cell in range(SIDE)
        for col_cell in range(SIDE)
    ]
    return jnp.stack(blocks, axis=1).reshape(-1, CELL_NODES, grid.shape[-1])


def add_cells(values, layers):
    width = values.shape[-1]
    side_nodes = SIDE * DEG + 1
    blocks = values.reshape(-1, SIDE, SIDE, EDGE, EDGE, EDGE, width)
    slabs = jnp.zeros((blocks.shape[0], EDGE, side_nodes, side_nodes, width), values.dtype)
    for row_cell in range(SIDE):
        for col_cell in range(SIDE):
            slabs = slabs.at[
                :, :, DEG * row_cell : DEG * row_cell + EDGE, DEG * col_cell : DEG * col_cell + EDGE
            ].add(blocks[:, row_cell, col_cell])
    lower = slabs[:, :DEG].reshape(layers, side_nodes, side_nodes, width)
    return (lower, slabs[:, DEG])


def per_device(
    orbitals,
    occupations,
    external,
    core_density,
    cell_scale,
    stiffness,
    touched_atom,
    touched_cells,
    projectors,
    coupling,
    atom_owner,
):
    n_cells = lax.axis_size(CELLS)
    node_dev, width = orbitals.shape
    total_nodes = node_dev * n_cells
    layers = THICK * DEG
    side_nodes = SIDE * DEG + 1
    here = lax.axis_index(CELLS)
    block = lax.axis_index("orb")
    proj_count = projectors.shape[2]
    atom_count = atom_owner.shape[0]
    owner = atom_owner[:, 0]
    atom_index = jnp.arange(atom_count, dtype=jnp.int32)
    earlier = (owner[None, :] == owner[:, None]) & (atom_index[None, :] < atom_index[:, None])
    owner_rank = jnp.sum(earlier.astype(jnp.int32), axis=1)
    own_slot = owner * OWN_CAP + owner_rank
    slot_all = jnp.sum(
        jnp.where(touched_atom[:, None] == atom_index[None, :], own_slot[None, :], 0), axis=1
    )
    my_slots = here * OWN_CAP + jnp.arange(OWN_CAP, dtype=jnp.int32)
    owned_hot = (slot_all[None, :] == my_slots[:, None]).astype(jnp.float32)
    flat_coupling = coupling.reshape(atom_count, proj_count * proj_count)
    mine = lax.dynamic_slice_in_dim(touched_atom, here * TOUCH_DEV, TOUCH_DEV)
    pair_hot = (mine[:, None] == touched_atom[None, :]).astype(jnp.float32)
    mine_pick = (mine[:, None] == atom_index[None, :]).astype(jnp.float32)
    mine_coupling = jnp.dot(mine_pick, flat_coupling, precision=highest).reshape(
        TOUCH_DEV, proj_count, proj_count
    )
    cell_hot = (
        touched_cells[:, :, None] == jnp.arange(CELL_DEV, dtype=jnp.int32)[None, None, :]
    ).astype(jnp.float32)
    spread = jnp.einsum("tqc,tqpn->tpcn", cell_hot, projectors, precision=highest).reshape(
        TOUCH_DEV * proj_count, CELL_DEV * CELL_NODES
    )
    columns = (
        jnp.arange(ORB, dtype=jnp.int32)[:, None]
        == block * width + jnp.arange(width, dtype=jnp.int32)[None, :]
    ).astype(jnp.float32)
    current = orbitals
    partial_density = jnp.dot(current * current, occupations, precision=highest)
    density = over_copies(partial_density, "orb")
    potential = external - exchange_coef * jnp.cbrt(density + core_density)
    grid = current.reshape(layers, side_nodes, side_nodes, width)
    upper_layer = passed_along(grid[0], CELLS, -1)
    cells = cut_cells(grid, upper_layer)
    local = cell_scale[:, None, None] * jnp.einsum(
        "mn,cnr->cmr", stiffness, cells, precision=highest
    )
    contrib = jnp.dot(
        spread, cells.reshape(CELL_DEV * CELL_NODES, width), precision=highest
    ).reshape(TOUCH_DEV, proj_count, width)
    piece = gather_axes(contrib, (("cells_0", "cells_1"), "cells_2"), 0)
    owned = jnp.einsum("kt,tpr->kpr", owned_hot, piece, precision=highest)
    touched_sums = jnp.einsum("kt,tpr->kpr", pair_hot, piece, precision=highest)
    returned = jnp.einsum("tpq,tqr->tpr", mine_coupling, touched_sums, precision=highest)
    nonlocal_term = jnp.einsum(
        "kn,kr->nr", spread, returned.reshape(TOUCH_DEV * proj_count, width), precision=highest
    ).reshape(CELL_DEV, CELL_NODES, width)
    lower, upper = add_cells(local + nonlocal_term, layers)
    lower = lower.at[DEG::DEG].add(upper[:-1])
    carried = passed_along(upper[-1], CELLS, 1)
    lower = lower.at[0].add(carried)
    image = lower.reshape(node_dev, width) + potential[:, None] * current
    numerator, denominator = packed_total(
        (jnp.sum(current * image, axis=0), jnp.sum(current * current, axis=0)), CELLS
    )
    rayleigh = numerator / (denominator + tiny)
    trial = current - step_size * (image - rayleigh[None, :] * current)
    everyone = lax.all_gather(trial, "orb", axis=1, tiled=True)
    partial_value = jnp.dot(trial.T, everyone, precision=highest) / total_nodes
    rows_summed = nested_sum(partial_value, CELLS)
    margin = lax.all_gather(rows_summed, "orb", axis=0, tiled=True)
    factor = jnp.linalg.cholesky(margin)
    weights = lax.linalg.triangular_solve(
        factor, columns, left_side=True, lower=True, transpose_a=True
    )
    current = jnp.dot(everyone, weights, precision=highest)
    return (current, rayleigh, owned)


def solution(mesh):
    finer = Mesh(
        mesh.devices.reshape(2, 8, 2, mesh.shape["orb"]), ("cells_0", "cells_1", "cells_2", "orb")
    )
    return jax.shard_map(
        per_device,
        mesh=finer,
        in_specs=(
            P(CELLS, "orb"),
            P("orb"),
            P(CELLS),
            P(CELLS),
            P(CELLS),
            P(),
            P(),
            P(CELLS, None),
            P(CELLS, None, None, None),
            P(),
            P(),
        ),
        out_specs=(P(CELLS, "orb"), P("orb"), P(CELLS, None, "orb")),
        check_vma=False,
    )
```

profile of v0, /device:TPU:1, one launch (start us, length us, event | category | flops | bytes accessed | tf_op | source)
XLA Modules:
  0.0 780.3 jit_solution(924222262672969636)
XLA Ops:
  10.4 7.5 all-to-all-start.2
  53.8 8.3 %all-to-all-start = ((f32[16,6,18,128]{3,1,2,0:T(8,128)}), f32[16,6,18,128]{3,1,2,0:T(8,128)S(1)}, u32[]{:S(2)}, u32[]{:S(2)}) async-start(f32[16,6,18,128]{3,1,2,0:T(8,128)} %broadcast_in_dim.23), calls=%async_computation | async-start | bytes 2359296 | tf_op jit(solution)/shard_map/all_to_all | solution.py:29
  75.2 14.6 %all-to-all-done = f32[16,6,18,128]{3,1,2,0:T(8,128)S(1)} async-done(((f32[16,6,18,128]{3,1,2,0:T(8,128)}), f32[16,6,18,128]{3,1,2,0:T(8,128)S(1)}, u32[]{:S(2)}, u32[]{:S(2)}) %all-to-all-start) | async-done | bytes 884768 | tf_op jit(solution)/shard_map/all_to_all | solution.py:29
  90.2 8.0 %all_to_all.32 = f32[2,16,6,18,128]{4,1,3,2,0:T(8,128)S(1)} all-to-all(f32[2,16,6,18,128]{4,1,3,2,0:T(8,128)S(1)} %broadcast_in_dim.24), channel_id=1, replica_groups=mesh['cells_0'=2,'cells_1'=8,'cells_2'=2,'orb'=8] {'cells_2'}, dimensions={0} | all-to-all | bytes 3538944 | tf_op jit(solution)/shard_map/all_to_all | solution.py:29
  103.7 6.4 bitcast_add_fusion.1
  155.6 15.4 %all_to_all.33 = f32[32,1,256]{2,1,0:T(1,128)S(1)} all-to-all(f32[32,1,256]{2,1,0:T(1,128)S(1)} %broadcast_in_dim.26), channel_id=1, replica_groups=mesh['cells_0'=2,'cells_1'=8,'cells_2'=2,'orb'=8] {'cells_0','cells_1','..., dimensions={0} | all-to-all | bytes 65536 | tf_op jit(solution)/shard_map/all_to_all | solution.py:29
  173.8 119.3 %all-gather.3.cloned.1.call-done = f32[2166,1024]{1,0:T(8,128)} async-done(((f32[2166,128]{1,0:T(8,128)}), f32[2166,1024]{1,0:T(8,128)}) %all-gather.3.cloned.1.call-update) | async-done | bytes 8871952 | tf_op jit(solution)/shard_map/all_gather | solution.py:197
  293.0 8.0 %convolution_multiply_fusion = f32[128,1024]{1,0:T(8,128)S(1)} fusion(f32[2166,128]{1,0:T(8,128)S(1)} %copy-done.5, f32[2166,1024]{1,0:T(8,128)} %all-gather.3.cloned.1.call-done), kind=kOutput, calls=%fused_computation.12 | convolution fusion | flops 3406954496 | bytes 10505216 | tf_op jit(solution)/shard_map/dot_general | solution.py:198
  301.2 25.0 %all_to_all.34 = f32[32,4,1024]{2,1,0:T(4,128)S(1)} all-to-all(f32[32,4,1024]{2,1,0:T(4,128)S(1)} %reshape.691), channel_id=1, replica_groups=mesh['cells_0'=2,'cells_1'=8,'cells_2'=2,'orb'=8] {'cells_0','cells_1','..., dimensions={0} | all-to-all | bytes 1048576 | tf_op jit(solution)/shard_map/all_to_all | solution.py:81
  326.3 21.4 %all_to_all.35 = f32[32,4,1024]{2,1,0:T(4,128)S(1)} all-to-all(f32[32,4,1024]{2,1,0:T(4,128)S(1)} %broadcast_in_dim.27), channel_id=1, replica_groups=mesh['cells_0'=2,'cells_1'=8,'cells_2'=2,'orb'=8] {'cells_0','cells_1','..., dimensions={0} | all-to-all | bytes 1048576 | tf_op jit(solution)/shard_map/all_to_all | solution.py:29
  350.8 71.2 %all-gather.5.cloned.1.call-done = f32[1024,1024]{0,1:T(8,128)} async-done(((f32[128,1024]{0,1:T(8,128)}), f32[1024,1024]{0,1:T(8,128)}) %all-gather.5.cloned.1.call-update) | async-done | bytes 4194320 | tf_op jit(solution)/shard_map/all_gather | solution.py:200
  422.0 5.5 copy.89
  427.5 4.4 fusion
  433.9 11.7 %cholesky.223 = f32[128,128]{1,0:T(8,128)S(1)} custom-call(f32[128,128]{1,0:T(8,128)S(1)} %cholesky.580), custom_call_target="Cholesky" | custom-call | tf_op jit(solution)/shard_map/jit(cholesky)/cholesky | solution.py:201
  448.8 9.8 %custom-call.62 = f32[1,128,128]{1,2,0:T(8,128)S(1)} custom-call(f32[1,128,128]{2,1,0:T(8,128)S(1)} %get-tuple-element.196), custom_call_target="InvertDiagBlocksLowerTriangular" | custom-call | tf_op jit(solution)/shard_map/jit(cholesky)/cholesky | solution.py:201
  462.5 11.9 %cholesky.244 = f32[128,128]{1,0:T(8,128)S(1)} custom-call(f32[128,128]{1,0:T(8,128)S(1)} %cholesky.584), custom_call_target="Cholesky" | custom-call | tf_op jit(solution)/shard_map/jit(cholesky)/cholesky | solution.py:201
  475.7 9.8 %custom-call.63 = f32[1,128,128]{1,2,0:T(8,128)S(1)} custom-call(f32[1,128,128]{2,1,0:T(8,128)S(1)} %get-tuple-element.193), custom_call_target="InvertDiagBlocksLowerTriangular" | custom-call | tf_op jit(solution)/shard_map/jit(cholesky)/cholesky | solution.py:201
  488.8 11.7 %cholesky.468 = f32[128,128]{1,0:T(8,128)S(1)} custom-call(f32[128,128]{1,0:T(8,128)S(1)} %cholesky.589), custom_call_target="Cholesky" | custom-call | tf_op jit(solution)/shard_map/jit(cholesky)/cholesky | solution.py:201
  501.8 9.8 %custom-call.64 = f32[1,128,128]{1,2,0:T(8,128)S(1)} custom-call(f32[1,128,128]{2,1,0:T(8,128)S(1)} %get-tuple-element.190), custom_call_target="InvertDiagBlocksLowerTriangular" | custom-call | tf_op jit(solution)/shard_map/jit(cholesky)/cholesky | solution.py:201
  515.2 12.1 %cholesky.487 = f32[128,128]{1,0:T(8,128)S(1)} custom-call(f32[128,128]{1,0:T(8,128)S(1)} %cholesky.594), custom_call_target="Cholesky" | custom-call | tf_op jit(solution)/shard_map/jit(cholesky)/cholesky | solution.py:201
  528.6 9.8 %custom-call.65 = f32[1,128,128]{1,2,0:T(8,128)S(1)} custom-call(f32[1,128,128]{2,1,0:T(8,128)S(1)} %get-tuple-element.187), custom_call_target="InvertDiagBlocksLowerTriangular" | custom-call | tf_op jit(solution)/shard_map/jit(cholesky)/cholesky | solution.py:201
  541.9 11.7 %cholesky.506 = f32[128,128]{1,0:T(8,128)S(1)} custom-call(f32[128,128]{1,0:T(8,128)S(1)} %cholesky.599), custom_call_target="Cholesky" | custom-call | tf_op jit(solution)/shard_map/jit(cholesky)/cholesky | solution.py:201
  555.0 9.9 %custom-call.66 = f32[1,128,128]{1,2,0:T(8,128)S(1)} custom-call(f32[1,128,128]{2,1,0:T(8,128)S(1)} %get-tuple-element.184), custom_call_target="InvertDiagBlocksLowerTriangular" | custom-call | tf_op jit(solution)/shard_map/jit(cholesky)/cholesky | solution.py:201
  568.2 11.7 %cholesky.526 = f32[128,128]{1,0:T(8,128)S(1)} custom-call(f32[128,128]{1,0:T(8,128)S(1)} %cholesky.604), custom_call_target="Cholesky" | custom-call | tf_op jit(solution)/shard_map/jit(cholesky)/cholesky | solution.py:201
  581.2 9.8 %custom-call.67 = f32[1,128,128]{1,2,0:T(8,128)S(1)} custom-call(f32[1,128,128]{2,1,0:T(8,128)S(1)} %get-tuple-element.181), custom_call_target="InvertDiagBlocksLowerTriangular" | custom-call | tf_op jit(solution)/shard_map/jit(cholesky)/cholesky | solution.py:201
  594.1 11.9 %cholesky.546 = f32[128,128]{1,0:T(8,128)S(1)} custom-call(f32[128,128]{1,0:T(8,128)S(1)} %cholesky.609), custom_call_target="Cholesky" | custom-call | tf_op jit(solution)/shard_map/jit(cholesky)/cholesky | solution.py:201
  607.3 9.8 %custom-call.68 = f32[1,128,128]{1,2,0:T(8,128)S(1)} custom-call(f32[1,128,128]{2,1,0:T(8,128)S(1)} %get-tuple-element.178), custom_call_target="InvertDiagBlocksLowerTriangular" | custom-call | tf_op jit(solution)/shard_map/jit(cholesky)/cholesky | solution.py:201
  619.7 11.7 %cholesky.564 = f32[128,128]{1,0:T(8,128)S(1)} custom-call(f32[128,128]{1,0:T(8,128)S(1)} %convolution_subtract_fusion.11), custom_call_target="Cholesky" | custom-call | tf_op jit(solution)/shard_map/jit(cholesky)/cholesky | solution.py:201
  637.9 4.9 select_select_fusion
  642.8 27.4 %while.11 = (s32[]{:T(128)}, f32[1024,1024]{1,0:T(8,128)}, s32[8,2]{0,1:T(2,128)S(1)}, f32[8,128,128]{2,1,0:T(8,128)}, s32[]{:T(128)}) while((s32[]{:T(128)}, f32[1024,1024]{1,0:T(8,128)}, s32[8,2]{0,1:T(2,128)S(1)}, f32[8,128,128]{2,1,0:T(8,128)}, s32[]{:T(128)}) %tuple.105), condition=%wide.while_cond.10, body=%wide.while_body.10.sunk | while | flops 2 | bytes 132205 | solution.py:202
  670.1 79.6 %custom-call.69 = f32[8,128,128]{1,2,0:T(8,128)S(1)} custom-call(f32[8,128,128]{2,1,0:T(8,128)} %get-tuple-element.130), custom_call_target="InvertDiagBlocksLowerTriangular" | custom-call | tf_op jit(solution)/shard_map/triangular_solve | solution.py:202
  762.6 10.4 %fusion.104 = f32[2166,128]{1,0:T(8,128)} fusion(f32[2166,1024]{1,0:T(8,128)} %all-gather.3.cloned.1.call-done, f32[1024,128]{1,0:T(8,128)S(1)} %constant_dynamic-update-slice_fusion.33), kind=kOutput, calls=%fused_computation.263 | convolution fusion | flops 3406823424 | bytes 10505216 | tf_op jit(solution)/shard_map/dot_general | solution.py:205
  (280 shorter events, 186.6 us)
Async XLA Ops:
  7.2 63.8 %copy-start = (f32[343,343]{1,0:T(8,128)S(1)}, f32[343,343]{1,0:T(8,128)}, u32[]{:S(2)}) copy-start(f32[343,343]{1,0:T(8,128)} %param.36) | copy-start | bytes 1411792
  7.2 10.7 %copy-start.2 = (f32[2166,128]{1,0:T(8,128)S(1)}, f32[2166,128]{1,0:T(8,128)}, u32[]{:S(2)}) copy-start(f32[2166,128]{1,0:T(8,128)} %param.31) | copy-start | bytes 3326980
  9.7 11.3 %copy-start.23 = (s32[6,1]{0,1:T(1,128)S(1)}, s32[6,1]{0,1:T(1,128)}, u32[]{:S(2)}) copy-start(s32[6,1]{0,1:T(1,128)} %param.38) | copy-start | bytes 76
  9.7 11.4 %copy-start.15 = (f32[6,1,18,343]{3,1,2,0:T(1,128)S(1)}, f32[6,1,18,343]{3,1,2,0:T(1,128)}, u32[]{:S(2)}) copy-start(f32[6,1,18,343]{3,1,2,0:T(1,128)} %param.39) | copy-start | bytes 444532
  10.4 27.7 %all-to-all-start.2 = ((f32[8,1,2166]{2,1,0:T(1,128)}), f32[8,1,2166]{2,1,0:T(1,128)}, u32[]{:S(2)}, u32[]{:S(2)}) async-start(f32[8,1,2166]{2,1,0:T(1,128)} %broadcast_in_dim.25), calls=%async_computation.2 | async-start | bytes 139264 | tf_op jit(solution)/shard_map/all_to_all | solution.py:29
  19.5 19.5 %collective-permute-start = (f32[19,19,128]{2,1,0:T(8,128)}, f32[19,19,128]{2,1,0:T(8,128)}, u32[]{:S(2)}, u32[]{:S(2)}) collective-permute-start(f32[19,19,128]{2,1,0:T(8,128)} %squeeze.4), channel_id=1, source_target_pairs={{0,248},{8,0},{16,8},{24,16},{32,24},{40,32},{48,40},{56,48},{64,5... | collective-permute-start | bytes 554504 | tf_op jit(solution)/shard_map/ppermute | solution.py:41
  25.1 4.5 copy-start.12
  25.1 4.6 copy-start.11
  30.4 4.2 copy-start.7
  30.4 5.6 copy-start.6
  33.9 2.2 copy-start.18
  33.9 2.3 copy-start.24
  34.7 2.9 copy-start.20
  52.6 9.7 %copy-start.16 = (f32[2166]{0:T(1024)S(1)}, f32[2166]{0:T(1024)}, u32[]{:S(2)}) copy-start(f32[2166]{0:T(1024)} %param.33) | copy-start | bytes 25996
  52.7 9.7 %copy-start.17 = (f32[2166]{0:T(1024)S(1)}, f32[2166]{0:T(1024)}, u32[]{:S(2)}) copy-start(f32[2166]{0:T(1024)} %param.34) | copy-start | bytes 25996
  53.8 36.0 %all-to-all-start = ((f32[16,6,18,128]{3,1,2,0:T(8,128)}), f32[16,6,18,128]{3,1,2,0:T(8,128)S(1)}, u32[]{:S(2)}, u32[]{:S(2)}) async-start(f32[16,6,18,128]{3,1,2,0:T(8,128)} %broadcast_in_dim.23), calls=%async_computation | async-start | bytes 2359296 | tf_op jit(solution)/shard_map/all_to_all | solution.py:29
  62.1 230.9 %all-gather.3.cloned.1.call-start = ((), (), s32[]{:S(2)}) async-start(), calls=%async_computation.6 | async-start | bytes 9990144 | tf_op jit(solution)/shard_map/all_gather | solution.py:197
  63.6 4.8 copy-start.10
  63.6 5.5 copy-start.9
  63.6 6.2 copy-start.8
  69.1 1.7 copy-start.13
  100.7 1.8 copy-start.19
  100.7 1.8 copy-start.21
  102.5 1.2 copy-start.22
  145.6 4.3 collective-permute-start.1
  149.5 4.5 copy-start.3
  171.1 2.6 copy-start.25
  173.7 119.4 %copy-start.5 = (f32[2166,128]{1,0:T(8,128)S(1)}, f32[2166,128]{1,0:T(8,128)}, u32[]{:S(2)}) copy-start(f32[2166,128]{1,0:T(8,128)} %multiply_subtract_fusion) | copy-start | bytes 3326980
  173.7 248.3 %all-gather.5.cloned.1.call-start = ((), (), s32[]{:S(2)}) async-start(), calls=%async_computation.7 | async-start | bytes 4718592 | tf_op jit(solution)/shard_map/all_gather | solution.py:200
  326.3 22.7 %copy-start.26 = (s32[64,1]{0,1:T(1,128)S(1)}, s32[64,1]{0,1:T(1,128)}, u32[]{:S(2)}) copy-start(s32[64,1]{0,1:T(1,128)} %param.41) | copy-start | bytes 772
  431.9 2.0 copy-start.4
  762.6 10.4 %copy-start.1 = (f32[343,343]{1,0:T(8,128)S(1)}, f32[343,343]{1,0:T(8,128)}, u32[]{:S(2)}) copy-start(f32[343,343]{1,0:T(8,128)} %param.36) | copy-start | bytes 1411792
  (1 other events, 0.9 us)
Sparse Core Ops, SparseCore 0:
  173.8 119.1 all-gather.2
  349.1 72.8 all-gather.4
where the time goes:
time: 789 us; the launch traced here: 780 us
  other arithmetic  284 us (36%)
  waiting for transfers between devices  206 us (26%)
  local copies, waits for them, and re-layouts  108 us (14%)
  matrix products  73.7 us (9%)
  blocking collectives  69.7 us (9%)
  between operations  20.7 us (3%)
  starting transfers between devices  18.4 us (2%)
    another operation x31, other arithmetic, per_device(): factor = jnp.linalg.cholesky(margin)  173 us
    all_gather x1, waiting for transfers between devices, per_device(): everyone = lax.all_gather(trial, 'orb', axis=1, tiled=True)  119 us
    another operation x3, other arithmetic, per_device(): lax.linalg.triangular_solve(factor, columns, left_side=True, lower=True,...  84.5 us
    all_gather x1, waiting for transfers between devices, per_device(): margin = lax.all_gather(rows_summed, 'orb', axis=0, tiled=True)  71.2 us
    all_to_all x3, blocking collectives, from_everyone(): lax.all_to_all(jnp.broadcast_to(value[None], (length, *value.shape)), axi...  44.8 us
    another operation x27, local copies, waits for them, and re-layouts  30.4 us
    all_to_all x1, blocking collectives, summed_on_arrival(): lax.all_to_all(parts, axis, split_axis=0, concat_axis=0, tiled=True)  25 us
    another operation x14, matrix products, per_device(): factor = jnp.linalg.cholesky(margin)  23.1 us
  transfers between devices with their start and end apart: 6, of which 4 were waited for; matrix products, arithmetic and copies ran while one was open for 5% of the time, Pallas kernels for 0%

commit v1 on v0

--- a/solution.py
+++ b/solution.py
@@ -1,8 +1,11 @@
+import functools
 import math
 
 import jax
 import jax.numpy as jnp
 from jax import lax
+from jax.experimental import pallas as pl
+from jax.experimental.pallas import tpu as pltpu
 from jax.sharding import Mesh
 from jax.sharding import PartitionSpec as P
 
@@ -15,7 +18,8 @@
 ORB = 1024
 TOUCH_DEV = 6
 OWN_CAP = 5
-CELLS = ("cells_0", "cells_1", "cells_2")
+CELLS = ("xl", "z", "core")
+ORBS = ("xh", "y")
 
 
 highest = lax.Precision.HIGHEST
@@ -59,34 +63,6 @@
         ends.append(ends[-1] + a.size)
     so_far = over_copies(jnp.concatenate([a.ravel() for a in arrays]), axis)
     return tuple((so_far[b:e].reshape(a.shape) for a, b, e in zip(arrays, ends, ends[1:])))
-
-
-def padded_to(lines, length):
-    spare = -len(lines) % length
-    return jnp.pad(lines, [(0, spare)] + [(0, 0)] * (lines.ndim - 1))
-
-
-def collect(value, axis, dim):
-    parts = from_everyone(value, axis)
-    return in_order(parts, dim)
-
-
-def cut_along(value, dim, length):
-    before, after = (value.shape[:dim], value.shape[dim + 1 :])
-    return jnp.moveaxis(value.reshape(*before, length, -1, *after), dim, 0)
-
-
-def summed_on_arrival(value, axis, dim):
-    parts = cut_along(value, dim, lax.axis_size(axis))
-    arrived = lax.all_to_all(parts, axis, split_axis=0, concat_axis=0, tiled=True)
-    return arrived.sum(axis=0)
-
-
-def nested_sum(value, axes):
-    lines = value.reshape(-1, value.shape[-1])
-    padded = padded_to(lines, lax.axis_size(axes))
-    whole = collect(summed_on_arrival(padded, axes, 0), axes, 0)
-    return lax.slice_in_dim(whole, 0, len(lines)).reshape(value.shape)
 
 
 def cut_cells(grid, upper_layer):
@@ -113,6 +89,336 @@
             ].add(blocks[:, row_cell, col_cell])
     lower = slabs[:, :DEG].reshape(layers, side_nodes, side_nodes, width)
     return (lower, slabs[:, DEG])
+
+
+ROWS = 272
+HALF = 18
+PIECE = 288
+SLOT = 18
+MESH_ID = pl.DeviceIdType.MESH
+WHOLE = pl.BlockSpec(memory_space=pltpu.VMEM)
+
+
+def split(x):
+    high = x.astype(jnp.bfloat16)
+    low = (x - high.astype(jnp.float32)).astype(jnp.bfloat16)
+    return high, low
+
+
+def orb_peer(index):
+    return {"xh": index // 4, "y": index % 4}
+
+
+def site_peer(index):
+    return {"xl": index // 8, "z": index % 8}
+
+
+def my_orb():
+    return lax.axis_index("xh") * 4 + lax.axis_index("y")
+
+
+def my_site():
+    return lax.axis_index("xl") * 8 + lax.axis_index("z")
+
+
+def greet(peers):
+    barrier = pltpu.get_barrier_semaphore()
+    for peer in peers:
+        pl.semaphore_signal(barrier, inc=1, device_id=peer, device_id_type=MESH_ID)
+    pl.semaphore_wait(barrier, len(peers))
+
+
+def remote(src, dst, send, recv, peer):
+    return pltpu.make_async_remote_copy(
+        src_ref=src, dst_ref=dst, send_sem=send, recv_sem=recv,
+        device_id=peer, device_id_type=MESH_ID,
+    )
+
+
+def rows_out_kernel(t_ref, out_ref, send, recv):
+    me = my_orb()
+    greet([orb_peer((me + r) % 8) for r in range(1, 8)])
+    copies = []
+    for r in (6, 2, 5, 3, 7, 1, 4):
+        peer = (me + r) % 8
+        copy = remote(t_ref.at[peer], out_ref.at[me], send.at[r], recv.at[r], orb_peer(peer))
+        copy.start()
+        copies.append(copy)
+    out_ref[me] = t_ref[me]
+    for copy in copies:
+        copy.wait()
+
+
+def exchange_rows(value, collective_id):
+    return pl.pallas_call(
+        rows_out_kernel,
+        out_shape=jax.ShapeDtypeStruct((8, ROWS, 128), jnp.float32),
+        in_specs=[WHOLE],
+        out_specs=WHOLE,
+        scratch_shapes=[pltpu.SemaphoreType.DMA((8,)), pltpu.SemaphoreType.DMA((8,))],
+        compiler_params=pltpu.CompilerParams(collective_id=collective_id, has_side_effects=True),
+    )(value)
+
+
+def gram_kernel(x_ref, out_ref, left_ref, right_ref):
+    for j in range(8):
+        high, low = split(x_ref[j])
+        lanes = pl.ds(128 * j, 128)
+        left_ref[0:ROWS, lanes] = high
+        left_ref[ROWS:2 * ROWS, lanes] = low
+        left_ref[2 * ROWS:3 * ROWS, lanes] = high
+        right_ref[0:ROWS, lanes] = high
+        right_ref[ROWS:2 * ROWS, lanes] = high
+        right_ref[2 * ROWS:3 * ROWS, lanes] = low
+    for i in range(8):
+        product = lax.dot_general(
+            left_ref[:, pl.ds(128 * i, 128)], right_ref[:, pl.ds(0, 128 * (i + 1))],
+            (((0,), (0,)), ((), ())), preferred_element_type=jnp.float32,
+        )
+        for j in range(i + 1):
+            out_ref[i * (i + 1) // 2 + j] = product[:, 128 * j:128 * (j + 1)]
+
+
+def gram(rows):
+    return pl.pallas_call(
+        gram_kernel,
+        out_shape=jax.ShapeDtypeStruct((36, 128, 128), jnp.float32),
+        in_specs=[WHOLE],
+        out_specs=WHOLE,
+        scratch_shapes=[pltpu.VMEM((3 * ROWS, 1024), jnp.bfloat16)] * 2,
+    )(rows)
+
+
+def total_kernel(
+    m_ref, out_ref, pair_ref, mine_ref, orb_ref, sum_ref, cut_ref, site_ref, done_ref,
+    pair_send, pair_recv, orb_send, orb_recv, site_send, site_recv,
+    back_send, back_recv, home_send, home_recv, last_send, last_recv,
+):
+    core = lax.axis_index("core")
+    me = my_orb()
+    here = my_site()
+    partner = {"core": 1 - core}
+    order = (6, 2, 5, 3, 7, 1, 4)
+    greet(
+        [partner]
+        + [orb_peer((me + r) % 8) for r in range(1, 8)]
+        + [site_peer((here + r) % 16) for r in range(1, 16)]
+    )
+    pending = []
+    arrivals = {}
+    for r in order + (0,):
+        piece = (me + r) % 8
+        copy = remote(
+            m_ref.at[1 - core, piece], pair_ref.at[piece], pair_send.at[r], pair_recv.at[r], partner
+        )
+        copy.start()
+        arrivals[r] = copy
+        pending.append(copy)
+    firsts = []
+    for r in order + (0,):
+        piece = (me + r) % 8
+        arrivals[r].wait_recv()
+        mine_ref[piece] = m_ref[core, piece] + pair_ref[piece]
+        if r:
+            copy = remote(mine_ref.at[piece], orb_ref.at[r], orb_send.at[r], orb_recv.at[r], orb_peer(piece))
+            copy.start()
+            firsts.append(copy)
+    total = mine_ref[me]
+    for copy, r in zip(firsts, order):
+        copy.wait_recv()
+        total = total + orb_ref[r]
+    sum_ref[...] = total
+    for i in range(16):
+        cut_ref[i] = sum_ref[SLOT * i:SLOT * (i + 1), :]
+    seconds = []
+    for r in range(1, 16):
+        peer = (here + r) % 16
+        copy = remote(cut_ref.at[peer], site_ref.at[r], site_send.at[r], site_recv.at[r], site_peer(peer))
+        copy.start()
+        seconds.append(copy)
+    slot = cut_ref[here]
+    for r, copy in enumerate(seconds, 1):
+        copy.wait_recv()
+        slot = slot + site_ref[r]
+    done_ref[here] = slot
+    thirds = []
+    for r in range(1, 16):
+        peer = (here + r) % 16
+        copy = remote(done_ref.at[here], done_ref.at[here], back_send.at[r], back_recv.at[r], site_peer(peer))
+        copy.start()
+        thirds.append(copy)
+    for copy in seconds:
+        copy.wait_send()
+    for copy in thirds:
+        copy.wait_recv()
+    for i in range(16):
+        sum_ref[SLOT * i:SLOT * (i + 1), :] = done_ref[i]
+    fourths = []
+    for r in order:
+        peer = (me + r) % 8
+        copy = remote(sum_ref, out_ref.at[core, me], home_send.at[r], home_recv.at[r], orb_peer(peer))
+        copy.start()
+        fourths.append(copy)
+    lasts = [remote(sum_ref, out_ref.at[core, me], last_send.at[0], last_recv.at[0], partner)]
+    lasts[0].start()
+    out_ref[core, me] = sum_ref[...]
+    for copy, r in zip(fourths, order):
+        source = (me + 8 - r) % 8
+        copy.wait_recv()
+        place = out_ref.at[core, source]
+        forward = remote(place, place, last_send.at[r], last_recv.at[r], partner)
+        forward.start()
+        lasts.append(forward)
+    for copy in pending + firsts + thirds + fourths + lasts:
+        copy.wait_send()
+    for copy in lasts:
+        copy.wait_recv()
+
+
+def total_blocks(blocks, collective_id):
+    pieces = blocks.reshape(2, 8, PIECE, 128)
+    eight = pltpu.SemaphoreType.DMA((8,))
+    sixteen = pltpu.SemaphoreType.DMA((16,))
+    total = pl.pallas_call(
+        total_kernel,
+        out_shape=jax.ShapeDtypeStruct(pieces.shape, jnp.float32),
+        in_specs=[WHOLE],
+        out_specs=WHOLE,
+        scratch_shapes=[
+            pltpu.VMEM((8, PIECE, 128), jnp.float32),
+            pltpu.VMEM((8, PIECE, 128), jnp.float32),
+            pltpu.VMEM((8, PIECE, 128), jnp.float32),
+            pltpu.VMEM((PIECE, 128), jnp.float32),
+            pltpu.VMEM((16, SLOT, 128), jnp.float32),
+            pltpu.VMEM((16, SLOT, 128), jnp.float32),
+            pltpu.VMEM((16, SLOT, 128), jnp.float32),
+            eight, eight, eight, eight, sixteen, sixteen,
+            sixteen, sixteen, eight, eight, eight, eight,
+        ],
+        compiler_params=pltpu.CompilerParams(collective_id=collective_id, has_side_effects=True),
+    )(pieces)
+    return total.reshape(36, 128, 128)
+
+
+def product(x, y):
+    xh, xl = split(x)
+    yh, yl = split(y)
+    right = jnp.concatenate([yh, yl], axis=1)
+    both = jnp.dot(
+        jnp.concatenate([xh, xl], axis=1), jnp.concatenate([right, right], axis=0),
+        preferred_element_type=jnp.float32,
+    )
+    return both[:, :128] + both[:, 128:]
+
+
+def twice(y):
+    yh, yl = split(y)
+    return jnp.concatenate(
+        [jnp.concatenate([yh, yh], axis=1), jnp.concatenate([yl, yl], axis=1)], axis=0
+    )
+
+
+def against(pair, right):
+    both = lax.dot_general(pair, right, (((1,), (1,)), ((), ())), preferred_element_type=jnp.float32)
+    return both[:, :128] + both[:, 128:]
+
+
+def pair_of(x):
+    return jnp.concatenate(split(x), axis=1)
+
+
+def solve_kernel(scale, m_ref, t_ref, out_ref, panel_ref, left_ref, inv_ref, work_ref, unit_ref):
+    row = lax.broadcasted_iota(jnp.int32, (128, 128), 0)
+    col = lax.broadcasted_iota(jnp.int32, (128, 128), 1)
+    eye = (row == col).astype(jnp.float32)
+    half = (row > col).astype(jnp.float32) + 0.5 * eye
+    down, across = [], []
+    for k in range(8):
+        diagonal = m_ref[k * (k + 1) // 2 + k] * eye
+        down.append(lax.rsqrt(jnp.sum(diagonal, axis=1, keepdims=True) * scale))
+        across.append(lax.rsqrt(jnp.sum(diagonal, axis=0, keepdims=True) * scale))
+    for j in range(8):
+        for i in range(j, 8):
+            block = m_ref[i * (i + 1) // 2 + j] * scale
+            panel_ref[j, 128 * i:128 * (i + 1), :] = block * down[i] * across[j]
+        panel_ref[j, 1024:1024 + ROWS, :] = t_ref[j] * across[j]
+    bottom = 1024 + ROWS
+    for k in range(8):
+        block = panel_ref[k, 128 * k:128 * (k + 1), :]
+        x = eye - half * (block - eye)
+        for step in range(2):
+            error = against(pair_of(product(x, block)), twice(x)) - eye
+            x = x - product(half * error, x)
+        inv_ref[...] = x
+        left = jnp.sum(jnp.sum(error * error, axis=0, keepdims=True), axis=1, keepdims=True)[0, 0]
+
+        @pl.when(jnp.logical_not(left < 1e-6))
+        def _():
+            work_ref[...] = panel_ref[k, 128 * k:128 * (k + 1), :]
+            unit_ref[...] = eye
+
+            def eliminate(j, carry):
+                lane = (col == j).astype(jnp.float32)
+                mine = work_ref[pl.ds(j, 1), :]
+                unit = unit_ref[pl.ds(j, 1), :]
+                pivot = jnp.sum(jnp.where(col[0:1] == j, mine, 0.0), axis=1, keepdims=True)
+                whole = work_ref[...]
+                column = jnp.sum(jnp.where(col == j, whole, 0.0), axis=1, keepdims=True)
+                factor = jnp.where(row > j, column / pivot, 0.0)
+                work_ref[...] = whole - factor * mine
+                unit_ref[...] = unit_ref[...] - factor * unit
+                inv_ref[pl.ds(j, 1), :] = unit * lax.rsqrt(pivot)
+                return carry
+
+            lax.fori_loop(0, 128, eliminate, 0)
+
+        right = twice(inv_ref[...])
+        starts = list(range(128 * (k + 1), 1024, 128)) + [1024, 1024 + ROWS // 2]
+        for start in starts:
+            size = 128 if start < 1024 else ROWS // 2
+            value = against(pair_of(panel_ref[k, start:start + size, :]), right)
+            if start < 1024:
+                left_ref[start:start + size, :] = pair_of(value)
+            else:
+                out_ref[k, start - 1024:start - 1024 + size, :] = value
+                if k < 7:
+                    left_ref[start:start + size, :] = pair_of(value)
+        for j in range(k + 1, 8):
+            pair = left_ref[128 * j:128 * (j + 1), :]
+            high, low = pair[:, :128], pair[:, 128:]
+            right = jnp.concatenate(
+                [jnp.concatenate([high, high], axis=1), jnp.concatenate([low, low], axis=1)], axis=0
+            )
+            for start in list(range(128 * j, 1024, 128)) + [1024, 1024 + ROWS // 2]:
+                size = 128 if start < 1024 else ROWS // 2
+                panel_ref[j, start:start + size, :] = panel_ref[j, start:start + size, :] - against(
+                    left_ref[start:start + size, :], right
+                )
+
+
+def solve_rows(blocks, rows, scale):
+    return pl.pallas_call(
+        functools.partial(solve_kernel, scale),
+        out_shape=jax.ShapeDtypeStruct((8, ROWS, 128), jnp.float32),
+        in_specs=[WHOLE, WHOLE],
+        out_specs=WHOLE,
+        scratch_shapes=[
+            pltpu.VMEM((8, 1024 + ROWS, 128), jnp.float32),
+            pltpu.VMEM((1024 + ROWS, 256), jnp.bfloat16),
+            pltpu.VMEM((128, 128), jnp.float32),
+            pltpu.VMEM((128, 128), jnp.float32),
+            pltpu.VMEM((128, 128), jnp.float32),
+        ],
+    )(blocks, rows)
+
+
+def orthonormal(trial, total_nodes):
+    padded = jnp.pad(trial, ((0, 8 * ROWS - trial.shape[0]), (0, 0)))
+    rows = exchange_rows(padded.reshape(8, ROWS, 128), 1)
+    blocks = total_blocks(gram(rows), 2)
+    solved = solve_rows(blocks, rows, 1.0 / total_nodes)
+    back = exchange_rows(solved, 3)
+    return back.reshape(8 * ROWS, 128)[: trial.shape[0]]
 
 
 def per_device(
@@ -134,7 +440,6 @@
     layers = THICK * DEG
     side_nodes = SIDE * DEG + 1
     here = lax.axis_index(CELLS)
-    block = lax.axis_index("orb")
     proj_count = projectors.shape[2]
     atom_count = atom_owner.shape[0]
     owner = atom_owner[:, 0]
@@ -160,13 +465,9 @@
     spread = jnp.einsum("tqc,tqpn->tpcn", cell_hot, projectors, precision=highest).reshape(
         TOUCH_DEV * proj_count, CELL_DEV * CELL_NODES
     )
-    columns = (
-        jnp.arange(ORB, dtype=jnp.int32)[:, None]
-        == block * width + jnp.arange(width, dtype=jnp.int32)[None, :]
-    ).astype(jnp.float32)
     current = orbitals
     partial_density = jnp.dot(current * current, occupations, precision=highest)
-    density = over_copies(partial_density, "orb")
+    density = over_copies(partial_density, ORBS)
     potential = external - exchange_coef * jnp.cbrt(density + core_density)
     grid = current.reshape(layers, side_nodes, side_nodes, width)
     upper_layer = passed_along(grid[0], CELLS, -1)
@@ -177,7 +478,7 @@
     contrib = jnp.dot(
         spread, cells.reshape(CELL_DEV * CELL_NODES, width), precision=highest
     ).reshape(TOUCH_DEV, proj_count, width)
-    piece = gather_axes(contrib, (("cells_0", "cells_1"), "cells_2"), 0)
+    piece = gather_axes(contrib, (("xl", "z"), "core"), 0)
     owned = jnp.einsum("kt,tpr->kpr", owned_hot, piece, precision=highest)
     touched_sums = jnp.einsum("kt,tpr->kpr", pair_hot, piece, precision=highest)
     returned = jnp.einsum("tpq,tqr->tpr", mine_coupling, touched_sums, precision=highest)
@@ -194,28 +495,18 @@
     )
     rayleigh = numerator / (denominator + tiny)
     trial = current - step_size * (image - rayleigh[None, :] * current)
-    everyone = lax.all_gather(trial, "orb", axis=1, tiled=True)
-    partial_value = jnp.dot(trial.T, everyone, precision=highest) / total_nodes
-    rows_summed = nested_sum(partial_value, CELLS)
-    margin = lax.all_gather(rows_summed, "orb", axis=0, tiled=True)
-    factor = jnp.linalg.cholesky(margin)
-    weights = lax.linalg.triangular_solve(
-        factor, columns, left_side=True, lower=True, transpose_a=True
-    )
-    current = jnp.dot(everyone, weights, precision=highest)
+    current = orthonormal(trial, total_nodes)
     return (current, rayleigh, owned)
 
 
 def solution(mesh):
-    finer = Mesh(
-        mesh.devices.reshape(2, 8, 2, mesh.shape["orb"]), ("cells_0", "cells_1", "cells_2", "orb")
-    )
+    finer = Mesh(mesh.devices.reshape(2, 8, 2, 2, 4), ("xl", "z", "core", "xh", "y"))
     return jax.shard_map(
         per_device,
         mesh=finer,
         in_specs=(
-            P(CELLS, "orb"),
-            P("orb"),
+            P(CELLS, ORBS),
+            P(ORBS),
             P(CELLS),
             P(CELLS),
             P(CELLS),
@@ -226,6 +517,6 @@
             P(),
             P(),
         ),
-        out_specs=(P(CELLS, "orb"), P("orb"), P(CELLS, None, "orb")),
+        out_specs=(P(CELLS, ORBS), P(ORBS), P(CELLS, None, ORBS)),
         check_vma=False,
     )

time: 789 us -> 397 us (0.50)
  other arithmetic: 284 us -> 21 us
  Pallas kernels: 0 us -> 224 us
  waiting for transfers between devices: 206 us -> 22.2 us
  blocking collectives: 69.7 us -> 7.99 us
  matrix products: 73.7 us -> 20.5 us
  local copies, waits for them, and re-layouts: 108 us -> 72 us
  between operations: 20.7 us -> 1.25 us
    another operation x39 -> x5, other arithmetic: 265 us -> 6.68 us  [the longest x31 173 us: per_device(): factor = jnp.linalg.cholesky(margin)]
    pallas_call x0 -> x5, Pallas kernels: none -> 224 us  [the longest x1 124 us: solve_rows(): pl.pallas_call(functools.partial(solve_kernel, scale), out_shape=jax.Shap...]
    all_gather x2 -> x0, waiting for transfers between devices: 190 us -> none  [the longest x1 119 us: per_device(): everyone = lax.all_gather(trial, 'orb', axis=1, tiled=True)]
    all_to_all x3 -> x1, blocking collectives: 44.8 us -> 7.99 us  [from_everyone(): lax.all_to_all(jnp.broadcast_to(value[None], (length, *value.shape)), axi...]
    another operation x29 -> x0, matrix products: 35.5 us -> none  [the longest x14 23.1 us: per_device(): factor = jnp.linalg.cholesky(margin)]
    another operation x40 -> x3, local copies, waits for them, and re-layouts: 32.9 us -> 3.06 us
    all_to_all x1 -> x0, blocking collectives: 25 us -> none  [summed_on_arrival(): lax.all_to_all(parts, axis, split_axis=0, concat_axis=0, tiled=True)]
    dot_general x2 -> x0, matrix products: 18.4 us -> none  [the longest x1 10.4 us: per_device(): current = jnp.dot(everyone, weights, precision=highest)]
  transfers between devices with their start and end apart: 6 -> 5, of which waited for: 4 -> 3; matrix products, arithmetic and copies ran while one was open for 5% -> 9% of each run, Pallas kernels for 0% -> 0%
where the time goes in v1:
time: 397 us; the launch traced here: 395 us
  Pallas kernels  224 us (56%)
  local copies, waits for them, and re-layouts  72 us (18%)
  starting transfers between devices  25.7 us (6%)
  waiting for transfers between devices  22.2 us (6%)
  other arithmetic  21 us (5%)
  matrix products  20.5 us (5%)
  blocking collectives  7.99 us (2%)
    pallas_call x1, Pallas kernels, solve_rows(): pl.pallas_call(functools.partial(solve_kernel, scale), out_shape=jax.Shap...  124 us
    pallas_call x1, Pallas kernels, total_blocks(): pl.pallas_call(total_kernel, out_shape=jax.ShapeDtypeStruct(pieces.shape,...  54 us
    pallas_call x2, Pallas kernels, exchange_rows(): pl.pallas_call(rows_out_kernel, out_shape=jax.ShapeDtypeStruct((8, ROWS,...  41.8 us
    all_to_all x3, starting transfers between devices, from_everyone(): lax.all_to_all(jnp.broadcast_to(value[None], (length, *value.shape)), axi...  23.6 us
    all_to_all x3, waiting for transfers between devices, from_everyone(): lax.all_to_all(jnp.broadcast_to(value[None], (length, *value.shape)), axi...  21.7 us
    scatter-add x9, local copies, waits for them, and re-layouts, add_cells(): slabs = slabs.at[:, :, DEG * row_cell:DEG * row_cell + EDGE, DEG * col_ce...  18.3 us
    all_to_all x1, blocking collectives, from_everyone(): lax.all_to_all(jnp.broadcast_to(value[None], (length, *value.shape)), axi...  7.99 us
  transfers between devices with their start and end apart: 5, of which 3 were waited for; matrix products, arithmetic and copies ran while one was open for 9% of the time, Pallas kernels for 0%

profile of v1, /device:TPU:1, one launch (start us, length us, event | category | flops | bytes accessed | tf_op | source)
XLA Modules:
  0.0 395.0 jit_solution(15967857598127865307)
XLA Ops:
  0.7 2.5 convolution_reduce_fusion
  3.8 7.6 %all-to-all-start.2 = ((f32[8,1,2166]{2,1,0:T(1,128)}), f32[8,1,2166]{2,1,0:T(1,128)}, u32[]{:S(2)}, u32[]{:S(2)}) async-start(f32[8,1,2166]{2,1,0:T(1,128)} %broadcast_in_dim.22), calls=%async_computation.2 | async-start | bytes 139264 | tf_op jit(solution)/shard_map/all_to_all | solution.py:33
  16.3 1.8 reshape.606
  24.6 3.4 reshape.636
  28.0 2.0 fusion.32
  40.3 2.5 reshape.630
  42.8 3.7 fusion.40
  47.7 8.3 %all-to-all-start = ((f32[16,6,18,128]{3,1,2,0:T(8,128)}), f32[16,6,18,128]{3,1,2,0:T(8,128)S(1)}, u32[]{:S(2)}, u32[]{:S(2)}) async-start(f32[16,6,18,128]{3,1,2,0:T(8,128)} %broadcast_in_dim.20), calls=%async_computation | async-start | bytes 2359296 | tf_op jit(solution)/shard_map/all_to_all | solution.py:33
  64.4 4.2 %fusion.5 = f32[9,128,343]{1,2,0:T(8,128)} fusion(f32[9,343,128]{2,1,0:T(8,128)S(1)} %constant_dynamic-update-slice_fusion.6, f32[343,343]{1,0:T(8,128)S(1)} %copy-done), kind=kOutput, calls=%fused_computation.12 | convolution fusion | flops 1626379776 | bytes 3631684 | tf_op jit(solution)/shard_map/mn,cnr->cmr/dot_general | solution.py:475
  68.6 15.1 %all-to-all-done = f32[16,6,18,128]{3,1,2,0:T(8,128)S(1)} async-done(((f32[16,6,18,128]{3,1,2,0:T(8,128)}), f32[16,6,18,128]{3,1,2,0:T(8,128)S(1)}, u32[]{:S(2)}, u32[]{:S(2)}) %all-to-all-start) | async-done | bytes 884768 | tf_op jit(solution)/shard_map/all_to_all | solution.py:33
  84.2 8.0 %all_to_all.22 = f32[2,16,6,18,128]{4,1,3,2,0:T(8,128)S(1)} all-to-all(f32[2,16,6,18,128]{4,1,3,2,0:T(8,128)S(1)} %broadcast_in_dim.21), channel_id=1, replica_groups=mesh['xl'=2,'z'=8,'core'=2,'xh'=2,'y'=4] {'core'}, dimensions={0} | all-to-all | bytes 3538944 | tf_op jit(solution)/shard_map/all_to_all | solution.py:33
  92.2 2.5 copy.75
  97.6 6.4 %bitcast_add_fusion = f32[9,343,128]{2,1,0:T(8,128)} fusion(f32[9,128,343]{1,2,0:T(8,128)} %fusion.5, f32[108,128,1]{1,0,2:T(8,128)S(1)} %reshape.632, f32[9,343,108]{1,0,2:T(8,128)} %reshape.636, f32[9]{0:T(128)S(1)} %copy-done.24), kind=kOutput, calls=%fused_computation.1 | convolution fusion | flops 512886528 | bytes 4550004 | tf_op jit(solution)/shard_map/kn,kr->nr/dot_general | solution.py:485
  104.0 2.6 reshape.608
  108.9 2.8 add_select_fusion.1
  111.7 3.0 scatter-add.35
  114.7 3.0 add_select_fusion
  117.8 3.0 scatter-add.36
  121.8 1.8 scatter-add.39
  124.8 1.8 scatter-add.40
  127.8 1.8 scatter-add.41
  136.6 1.8 scatter-add.46
  140.6 2.5 slice_bitcast_fusion
  145.2 2.3 reshape.623
  149.9 7.6 %all-to-all-start.3 = ((f32[32,1,256]{2,1,0:T(1,128)}), f32[32,1,256]{2,1,0:T(1,128)S(1)}, u32[]{:S(2)}, u32[]{:S(2)}) async-start(f32[32,1,256]{2,1,0:T(1,128)} %broadcast_in_dim.23), calls=%async_computation.3 | async-start | bytes 65536 | tf_op jit(solution)/shard_map/all_to_all | solution.py:33
  158.9 6.6 %all-to-all-done.3 = f32[32,1,256]{2,1,0:T(1,128)S(1)} async-done(((f32[32,1,256]{2,1,0:T(1,128)}), f32[32,1,256]{2,1,0:T(1,128)S(1)}, u32[]{:S(2)}, u32[]{:S(2)}) %all-to-all-start.3) | async-done | bytes 32800 | tf_op jit(solution)/shard_map/all_to_all | solution.py:33
  168.3 22.7 %shard_map.130.x_ref.t_ref = f32[8,272,128]{2,1,0:T(8,128)} custom-call(f32[8,272,128]{2,1,0:T(8,128)} %bitcast.123), custom_call_target="tpu_custom_call" | custom-call | tf_op jit(solution)/shard_map/pallas_call | solution.py:153
  191.1 4.8 %shard_map.131 = f32[36,128,128]{2,1,0:T(8,128)} custom-call(f32[8,272,128]{2,1,0:T(8,128)} %shard_map.130.x_ref.t_ref), custom_call_target="tpu_custom_call" | custom-call | tf_op jit(solution)/shard_map/pallas_call | solution.py:183
  195.9 54.0 %shard_map.132 = f32[2,8,288,128]{3,2,1,0:T(8,128)} custom-call(f32[2,8,288,128]{3,2,1,0:T(8,128)} %bitcast.120), custom_call_target="tpu_custom_call" | custom-call | tf_op jit(solution)/shard_map/pallas_call | solution.py:282
  250.0 123.6 %shard_map.133.t_ref = f32[8,272,128]{2,1,0:T(8,128)} custom-call(f32[36,128,128]{2,1,0:T(8,128)} %bitcast.119, f32[8,272,128]{2,1,0:T(8,128)} %shard_map.130.x_ref.t_ref), custom_call_target="tpu_custom_call" | custom-call | tf_op jit(solution)/shard_map/pallas_call | solution.py:400
  373.6 19.1 %shard_map.134 = f32[8,272,128]{2,1,0:T(8,128)} custom-call(f32[8,272,128]{2,1,0:T(8,128)} %shard_map.133.t_ref), custom_call_target="tpu_custom_call" | custom-call | tf_op jit(solution)/shard_map/pallas_call | solution.py:153
  392.7 2.3 slice.554
  (155 shorter events, 58.0 us)
Async XLA Ops:
  0.6 63.8 %copy-start = (f32[343,343]{1,0:T(8,128)S(1)}, f32[343,343]{1,0:T(8,128)}, u32[]{:S(2)}) copy-start(f32[343,343]{1,0:T(8,128)} %param.36) | copy-start | bytes 1411792
  0.6 10.8 %copy-start.1 = (f32[2166,128]{1,0:T(8,128)S(1)}, f32[2166,128]{1,0:T(8,128)}, u32[]{:S(2)}) copy-start(f32[2166,128]{1,0:T(8,128)} %param.31) | copy-start | bytes 3326980
  3.8 10.2 %copy-start.25 = (s32[6,1]{0,1:T(1,128)S(1)}, s32[6,1]{0,1:T(1,128)}, u32[]{:S(2)}) copy-start(s32[6,1]{0,1:T(1,128)} %param.38) | copy-start | bytes 76
  3.8 10.3 %copy-start.15 = (f32[6,1,18,343]{3,1,2,0:T(1,128)S(1)}, f32[6,1,18,343]{3,1,2,0:T(1,128)}, u32[]{:S(2)}) copy-start(f32[6,1,18,343]{3,1,2,0:T(1,128)} %param.39) | copy-start | bytes 444532
  3.8 28.3 %all-to-all-start.2 = ((f32[8,1,2166]{2,1,0:T(1,128)}), f32[8,1,2166]{2,1,0:T(1,128)}, u32[]{:S(2)}, u32[]{:S(2)}) async-start(f32[8,1,2166]{2,1,0:T(1,128)} %broadcast_in_dim.22), calls=%async_computation.2 | async-start | bytes 139264 | tf_op jit(solution)/shard_map/all_to_all | solution.py:33
  13.1 20.0 %collective-permute-start = (f32[19,19,128]{2,1,0:T(8,128)}, f32[19,19,128]{2,1,0:T(8,128)}, u32[]{:S(2)}, u32[]{:S(2)}) collective-permute-start(f32[19,19,128]{2,1,0:T(8,128)} %squeeze.4), channel_id=1, source_target_pairs={{0,248},{8,0},{16,8},{24,16},{32,24},{40,32},{48,40},{56,48},{64,5... | collective-permute-start | bytes 554504 | tf_op jit(solution)/shard_map/ppermute | solution.py:45
  14.0 5.6 %copy-start.18 = (s32[2]{0:T(128)}, s32[2]{0:T(128)S(1)}, u32[]{:S(2)}) copy-start(s32[2]{0:T(128)S(1)} %get-tuple-element.161) | copy-start | bytes 28
  16.3 1.9 copy-start.29
  16.3 2.0 copy-start.20
  18.1 5.6 %copy-start.11 = (f32[361,128]{1,0:T(8,128)S(1)}, f32[361,128]{1,0:T(8,128)}, u32[]{:S(2)}) copy-start(f32[361,128]{1,0:T(8,128)} %get-tuple-element.153) | copy-start | bytes 554500
  18.1 5.6 %copy-start.10 = (f32[361,128]{1,0:T(8,128)S(1)}, f32[361,128]{1,0:T(8,128)}, u32[]{:S(2)}) copy-start(f32[361,128]{1,0:T(8,128)} %get-tuple-element.154) | copy-start | bytes 554500
  18.1 5.7 %copy-start.9 = (f32[361,128]{1,0:T(8,128)S(1)}, f32[361,128]{1,0:T(8,128)}, u32[]{:S(2)}) copy-start(f32[361,128]{1,0:T(8,128)} %get-tuple-element.155) | copy-start | bytes 554500
  24.5 3.4 copy-start.4
  24.5 5.4 %copy-start.3 = (f32[1,1,19,19,128]{4,3,2,1,0:T(8,128)S(1)}, f32[1,1,19,19,128]{4,3,2,1,0:T(8,128)}, u32[]{:S(2)}) copy-start(f32[1,1,19,19,128]{4,3,2,1,0:T(8,128)} %stack.72) | copy-start | bytes 554500
  28.0 2.1 copy-start.19
  28.0 2.1 copy-start.26
  46.6 9.5 %copy-start.16 = (f32[2166]{0:T(1024)S(1)}, f32[2166]{0:T(1024)}, u32[]{:S(2)}) copy-start(f32[2166]{0:T(1024)} %param.33) | copy-start | bytes 25996
  46.6 9.5 %copy-start.17 = (f32[2166]{0:T(1024)S(1)}, f32[2166]{0:T(1024)}, u32[]{:S(2)}) copy-start(f32[2166]{0:T(1024)} %param.34) | copy-start | bytes 25996
  47.7 36.0 %all-to-all-start = ((f32[16,6,18,128]{3,1,2,0:T(8,128)}), f32[16,6,18,128]{3,1,2,0:T(8,128)S(1)}, u32[]{:S(2)}, u32[]{:S(2)}) async-start(f32[16,6,18,128]{3,1,2,0:T(8,128)} %broadcast_in_dim.20), calls=%async_computation | async-start | bytes 2359296 | tf_op jit(solution)/shard_map/all_to_all | solution.py:33
  57.3 3.9 copy-start.8
  57.3 4.6 %copy-start.7 = (f32[1,7,7,7,128]{4,3,2,1,0:T(8,128)S(1)}, f32[1,7,7,7,128]{4,3,2,1,0:T(8,128)}, u32[]{:S(2)}) copy-start(f32[1,7,7,7,128]{4,3,2,1,0:T(8,128)} %get-tuple-element.147) | copy-start | bytes 526852
  57.3 5.3 %copy-start.6 = (f32[1,7,7,7,128]{4,3,2,1,0:T(8,128)S(1)}, f32[1,7,7,7,128]{4,3,2,1,0:T(8,128)}, u32[]{:S(2)}) copy-start(f32[1,7,7,7,128]{4,3,2,1,0:T(8,128)} %get-tuple-element.148) | copy-start | bytes 526852
  57.3 6.0 %copy-start.5 = (f32[1,7,7,7,128]{4,3,2,1,0:T(8,128)S(1)}, f32[1,7,7,7,128]{4,3,2,1,0:T(8,128)}, u32[]{:S(2)}) copy-start(f32[1,7,7,7,128]{4,3,2,1,0:T(8,128)} %get-tuple-element.149) | copy-start | bytes 526852
  61.8 2.4 copy-start.12
  62.5 1.7 copy-start.13
  94.7 1.8 copy-start.21
  94.7 1.8 copy-start.23
  139.4 4.2 %collective-permute-start.1 = (f32[19,19,128]{2,1,0:T(8,128)S(1)}, f32[19,19,128]{2,1,0:T(8,128)S(1)}, u32[]{:S(2)}, u32[]{:S(2)}) collective-permute-start(f32[19,19,128]{2,1,0:T(8,128)S(1)} %slice_bitcast_fusion.1), channel_id=1, source_target_pairs={{0,8},{8,16},{16,24},{24,32},{32,40},{40,48},{48,56},{56,64},{64,7... | collective-permute-start | bytes 554504 | tf_op jit(solution)/shard_map/ppermute | solution.py:45
  143.1 4.5 %copy-start.2 = (f32[2166,128]{1,0:T(8,128)S(1)}, f32[2166,128]{1,0:T(8,128)}, u32[]{:S(2)}) copy-start(f32[2166,128]{1,0:T(8,128)} %param.31) | copy-start | bytes 3326980
  147.6 9.9 %copy-start.22 = (s32[192]{0:T(256)S(1)}, s32[192]{0:T(256)}, u32[]{:S(2)}) copy-start(s32[192]{0:T(256)} %select_reduce_fusion) | copy-start | bytes 2308
  147.6 9.9 %copy-start.27 = (s32[5]{0:T(128)S(1)}, s32[5]{0:T(128)}, u32[]{:S(2)}) copy-start(s32[5]{0:T(128)} %iota_add_fusion) | copy-start | bytes 64
  149.9 15.6 %all-to-all-start.3 = ((f32[32,1,256]{2,1,0:T(1,128)}), f32[32,1,256]{2,1,0:T(1,128)S(1)}, u32[]{:S(2)}, u32[]{:S(2)}) async-start(f32[32,1,256]{2,1,0:T(1,128)} %broadcast_in_dim.23), calls=%async_computation.3 | async-start | bytes 65536 | tf_op jit(solution)/shard_map/all_to_all | solution.py:33
  (3 other events, 3.7 us)

commit v2 on v1

--- a/solution.py
+++ b/solution.py
@@ -13,86 +13,21 @@
 EDGE = 7
 CELL_NODES = 343
 SIDE = 3
-THICK = 1
-CELL_DEV = 9
-ORB = 1024
+PROJ = 18
+ATOM_DEV = 2
+REACH = 2
 TOUCH_DEV = 6
 OWN_CAP = 5
 CELLS = ("xl", "z", "core")
 ORBS = ("xh", "y")
 
-
 highest = lax.Precision.HIGHEST
 step_size = 0.1
 exchange_coef = (3.0 / math.pi) ** (1.0 / 3.0)
 tiny = 1e-06
 
 
-def from_everyone(value, axis):
-    length = lax.axis_size(axis)
-    return lax.all_to_all(
-        jnp.broadcast_to(value[None], (length, *value.shape)), axis, 0, 0, tiled=True
-    )
-
-
-def over_copies(value, axis):
-    return from_everyone(value, axis).sum(axis=0)
-
-
-def passed_along(value, axis, steps):
-    count = lax.axis_size(axis)
-    pairs = [(source, (source + steps) % count) for source in range(count)]
-    return lax.ppermute(value, axis, pairs)
-
-
-def in_order(parts, dim):
-    lengths = list(parts.shape[1:])
-    lengths[dim] *= parts.shape[0]
-    return jnp.moveaxis(parts, 0, dim).reshape(lengths)
-
-
-def gather_axes(value, axes, dim):
-    far, near = axes
-    parts = from_everyone(from_everyone(value, far), near)
-    return in_order(parts.swapaxes(0, 1).reshape(-1, *value.shape), dim)
-
-
-def packed_total(arrays, axis):
-    ends = [0]
-    for a in arrays:
-        ends.append(ends[-1] + a.size)
-    so_far = over_copies(jnp.concatenate([a.ravel() for a in arrays]), axis)
-    return tuple((so_far[b:e].reshape(a.shape) for a, b, e in zip(arrays, ends, ends[1:])))
-
-
-def cut_cells(grid, upper_layer):
-    layers = grid.shape[0]
-    extended = jnp.concatenate([grid, upper_layer[None]], axis=0)
-    slabs = jnp.stack([extended[offset : offset + layers : DEG] for offset in range(EDGE)], axis=1)
-    blocks = [
-        slabs[:, :, DEG * row_cell : DEG * row_cell + EDGE, DEG * col_cell : DEG * col_cell + EDGE]
-        for row_cell in range(SIDE)
-        for col_cell in range(SIDE)
-    ]
-    return jnp.stack(blocks, axis=1).reshape(-1, CELL_NODES, grid.shape[-1])
-
-
-def add_cells(values, layers):
-    width = values.shape[-1]
-    side_nodes = SIDE * DEG + 1
-    blocks = values.reshape(-1, SIDE, SIDE, EDGE, EDGE, EDGE, width)
-    slabs = jnp.zeros((blocks.shape[0], EDGE, side_nodes, side_nodes, width), values.dtype)
-    for row_cell in range(SIDE):
-        for col_cell in range(SIDE):
-            slabs = slabs.at[
-                :, :, DEG * row_cell : DEG * row_cell + EDGE, DEG * col_cell : DEG * col_cell + EDGE
-            ].add(blocks[:, row_cell, col_cell])
-    lower = slabs[:, :DEG].reshape(layers, side_nodes, side_nodes, width)
-    return (lower, slabs[:, DEG])
-
-
 ROWS = 272
-HALF = 18
 PIECE = 288
 SLOT = 18
 MESH_ID = pl.DeviceIdType.MESH
@@ -350,9 +285,20 @@
             error = against(pair_of(product(x, block)), twice(x)) - eye
             x = x - product(half * error, x)
         inv_ref[...] = x
-        left = jnp.sum(jnp.sum(error * error, axis=0, keepdims=True), axis=1, keepdims=True)[0, 0]
-
-        @pl.when(jnp.logical_not(left < 1e-6))
+
+        def unfinished(state):
+            return (state[0] < 12) & jnp.logical_not(state[1] < 3e-5)
+
+        def improve(state):
+            x = inv_ref[...]
+            block = panel_ref[k, 128 * k:128 * (k + 1), :]
+            error = against(pair_of(product(x, block)), twice(x)) - eye
+            inv_ref[...] = x - product(half * error, x)
+            return state[0] + 1, jnp.sum(error * error)
+
+        left = lax.while_loop(unfinished, improve, (0, jnp.sum(error * error)))[1]
+
+        @pl.when(jnp.logical_not(left < 3e-5))
         def _():
             work_ref[...] = panel_ref[k, 128 * k:128 * (k + 1), :]
             unit_ref[...] = eye
@@ -412,13 +358,351 @@
     )(blocks, rows)
 
 
-def orthonormal(trial, total_nodes):
-    padded = jnp.pad(trial, ((0, 8 * ROWS - trial.shape[0]), (0, 0)))
-    rows = exchange_rows(padded.reshape(8, ROWS, 128), 1)
-    blocks = total_blocks(gram(rows), 2)
-    solved = solve_rows(blocks, rows, 1.0 / total_nodes)
-    back = exchange_rows(solved, 3)
-    return back.reshape(8 * ROWS, 128)[: trial.shape[0]]
+WINDOW = 2 * REACH + 1
+TILE = 8
+LINES = SIDE * DEG + 1
+PLANE = LINES * LINES
+HALO = 368
+PADDED = EDGE * EDGE * TILE
+
+
+def cell_peer(index):
+    return {"xl": index // 16, "z": (index // 2) % 8, "core": index % 2}
+
+
+def thrice(left, right, dims):
+    lh, ll = left
+    rh, rl = right
+    dot = functools.partial(
+        lax.dot_general, dimension_numbers=(dims, ((), ())), preferred_element_type=jnp.float32
+    )
+    return dot(lh, rh) + dot(ll, rh) + dot(lh, rl)
+
+
+def cube_root(x):
+    root = jnp.exp(jnp.log(x) * (1.0 / 3.0))
+    for _ in range(2):
+        root = root - (root * root * root - x) / (3.0 * root * root)
+    return root
+
+
+def trial_kernel(
+    scale_ref, hot_ref,
+    c_ref, occ_ref, ext_ref, core_ref, stiff_ref, proj_ref, coup_ref,
+    rows_ref, ray_ref, sums_ref,
+    halo_ref, tile_ref, value_ref, image_ref, top_ref, under_ref, proj24_ref,
+    give_ref, take_ref, used_ref, window_ref, dens_ref, ray_all_ref, pot_ref,
+    halo_sem, dens_send, dens_recv, give_send, give_recv, used_send, used_recv,
+    top_sem, ray_send, ray_recv, rows_send, rows_recv, sums_send, sums_recv,
+):
+    nodes = c_ref.shape[0]
+    here = lax.axis_index("xl") * 16 + lax.axis_index("z") * 2 + lax.axis_index("core")
+    me = my_orb()
+    barrier = pltpu.get_barrier_semaphore()
+    peers = [cell_peer((here + r) % 32) for r in range(1, 32)]
+    peers += [orb_peer((me + r) % 8) for r in range(1, 8)]
+    for peer in peers:
+        pl.semaphore_signal(barrier, inc=1, device_id=peer, device_id_type=MESH_ID)
+    sends = []
+
+    current = c_ref[...]
+    square = current * current
+    occ = occ_ref[...]
+    density = thrice(split(jnp.broadcast_to(occ, (TILE, 128))), split(square), ((1,), (1,)))
+    dens_ref[0] = density[0:1, :]
+
+    node = lax.broadcasted_iota(jnp.int32, (CELL_NODES, PADDED), 0)
+    place = lax.broadcasted_iota(jnp.int32, (CELL_NODES, PADDED), 1)
+    inside = (place & 7) < EDGE
+    match = node == EDGE * (place >> 3) + (place & 7)
+    spot = jnp.where(inside & match, 1.0, 0.0).astype(jnp.bfloat16)
+    dot = functools.partial(lax.dot_general, preferred_element_type=jnp.float32)
+
+    def both_sides(part):
+        wide = dot(part, spot, (((1,), (0,)), ((), ()))).astype(jnp.bfloat16)
+        return dot(spot, wide, (((0,), (0,)), ((), ()))).astype(jnp.bfloat16)
+
+    stiff = tuple(both_sides(part) for part in split(stiff_ref[...]))
+    proj24_ref[...] = jnp.zeros_like(proj24_ref)
+    for t in range(TOUCH_DEV):
+        proj24_ref[24 * t:24 * t + PROJ, :] = proj_ref[t, 0]
+    parts = split(proj24_ref[...])
+    proj_rows = tuple(dot(p, spot, (((1,), (0,)), ((), ()))).astype(jnp.bfloat16) for p in parts)
+    proj_cols = tuple(dot(spot, p, (((0,), (1,)), ((), ()))).astype(jnp.bfloat16) for p in parts)
+
+    pl.semaphore_wait(barrier, len(peers))
+    halo = remote(
+        c_ref.at[pl.ds(0, HALO)], halo_ref, halo_sem.at[0], halo_sem.at[1], cell_peer((here + 31) % 32)
+    )
+    halo.start()
+    dens_copies = []
+    for r in range(1, 8):
+        peer = (me + r) % 8
+        copy = remote(dens_ref.at[0], dens_ref.at[r], dens_send.at[r], dens_recv.at[r], orb_peer(peer))
+        copy.start()
+        dens_copies.append(copy)
+
+    for a in range(DEG):
+        for y in range(LINES):
+            for s in range(SIDE):
+                start = PLANE * a + LINES * y + DEG * s
+                if start + TILE > nodes:
+                    piece = jnp.concatenate(
+                        [c_ref[start:nodes, :], jnp.zeros((start + TILE - nodes, 128), jnp.float32)], axis=0
+                    )
+                else:
+                    piece = c_ref[start:start + TILE, :]
+                tile_ref[s, a, TILE * y:TILE * (y + 1), :] = piece
+    halo.wait_recv()
+    for y in range(LINES):
+        for s in range(SIDE):
+            start = LINES * y + DEG * s
+            tile_ref[s, DEG, TILE * y:TILE * (y + 1), :] = halo_ref[start:start + TILE, :]
+
+    def cell_values(r):
+        span = slice(DEG * TILE * r, DEG * TILE * r + EDGE * TILE)
+        return [
+            jnp.concatenate([tile_ref[s, a, span, :] for a in range(EDGE)], axis=0)
+            for s in range(SIDE)
+        ]
+
+    contrib = [jnp.zeros((24, 128), jnp.float32) for _ in range(TOUCH_DEV)]
+    for r in range(SIDE):
+        wide = thrice(proj_rows, split(jnp.concatenate(cell_values(r), axis=1)), ((1,), (0,)))
+        for t in range(TOUCH_DEV):
+            for s in range(SIDE):
+                part = wide[24 * t:24 * t + 24, 128 * s:128 * (s + 1)]
+                contrib[t] = contrib[t] + hot_ref[t, 10 + SIDE * r + s] * part
+    for k in range(WINDOW):
+        for m in range(ATOM_DEV):
+            total = hot_ref[0, ATOM_DEV * k + m] * contrib[0]
+            for t in range(1, TOUCH_DEV):
+                total = total + hot_ref[t, ATOM_DEV * k + m] * contrib[t]
+            give_ref[k, m] = total[:PROJ]
+    gives = {}
+    for k in (0, 4, 1, 3):
+        copy = remote(
+            give_ref.at[k], take_ref.at[k], give_send.at[k], give_recv.at[k],
+            cell_peer((here + k + 32 - REACH) % 32),
+        )
+        copy.start()
+        gives[k] = copy
+
+    value_ref[...] = jnp.zeros_like(value_ref)
+
+    def add_value(r, wide):
+        for s in range(SIDE):
+            for a in range(EDGE):
+                span = slice(DEG * TILE * r, DEG * TILE * r + EDGE * TILE)
+                value_ref[s, a, span, :] = (
+                    value_ref[s, a, span, :]
+                    + wide[EDGE * TILE * a:EDGE * TILE * (a + 1), 128 * s:128 * (s + 1)]
+                )
+
+    for r in range(SIDE):
+        wide = jnp.concatenate(
+            [value * scale_ref[SIDE * r + s] for s, value in enumerate(cell_values(r))], axis=1
+        )
+        add_value(r, thrice(stiff, split(wide), ((1,), (0,))))
+
+    for k in (0, 4, 1, 3):
+        gives[k].wait_recv()
+    useds = {}
+    for m in range(ATOM_DEV):
+        total = give_ref[REACH, m]
+        for k in (0, 1, 3, 4):
+            total = total + take_ref[k, m]
+        sums_ref[here, m] = total
+        used_ref[m] = thrice(split(coup_ref[2 * here + m]), split(total), ((1,), (0,)))
+        window_ref[REACH, m] = used_ref[m]
+    for q in (0, 4, 1, 3):
+        copy = remote(
+            used_ref, window_ref.at[4 - q], used_send.at[4 - q], used_recv.at[4 - q],
+            cell_peer((here + q + 32 - REACH) % 32),
+        )
+        copy.start()
+        useds[4 - q] = copy
+
+    for copy in dens_copies:
+        copy.wait_recv()
+    density = dens_ref[0]
+    for r in range(1, 8):
+        density = density + dens_ref[r]
+    potential = ext_ref[...] - exchange_coef * cube_root(density + core_ref[...])
+    pot_ref[...] = dot(
+        jnp.broadcast_to(potential, (TILE, nodes)),
+        (lax.broadcasted_iota(jnp.int32, (TILE, 128), 0) == 0).astype(jnp.float32),
+        (((0,), (0,)), ((), ())), precision=highest,
+    )
+
+    for k in (0, 4, 1, 3):
+        useds[k].wait_recv()
+    back = []
+    for t in range(TOUCH_DEV):
+        total = jnp.zeros((PROJ, 128), jnp.float32)
+        for k in range(WINDOW):
+            for m in range(ATOM_DEV):
+                total = total + hot_ref[t, ATOM_DEV * k + m] * window_ref[k, m]
+        back.append(jnp.concatenate([total, jnp.zeros((24 - PROJ, 128), jnp.float32)], axis=0))
+    for r in range(SIDE):
+        wide = jnp.concatenate(
+            [
+                jnp.concatenate(
+                    [
+                        hot_ref[t, 10 + SIDE * r + s] * back[t]
+                        for t in range(TOUCH_DEV)
+                    ],
+                    axis=0,
+                )
+                for s in range(SIDE)
+            ],
+            axis=1,
+        )
+        add_value(r, thrice(proj_cols, split(wide), ((1,), (0,))))
+
+    top_ref[...] = jnp.zeros_like(top_ref)
+    for y in range(LINES):
+        for s in range(SIDE):
+            start = LINES * y + DEG * s
+            top_ref[start:start + TILE, :] = (
+                top_ref[start:start + TILE, :] + value_ref[s, DEG, TILE * y:TILE * (y + 1), :]
+            )
+    top = remote(top_ref, under_ref, top_sem.at[0], top_sem.at[1], cell_peer((here + 1) % 32))
+    top.start()
+
+    current = c_ref[...]
+    square = current * current
+    numerator = jnp.sum(pot_ref[...] * square, axis=0, keepdims=True)
+    for s in range(SIDE):
+        for a in range(EDGE):
+            numerator = numerator + jnp.sum(tile_ref[s, a] * value_ref[s, a], axis=0, keepdims=True)
+    ray_all_ref[here, 0:1, :] = numerator
+    ray_all_ref[here, 1:2, :] = jnp.sum(square, axis=0, keepdims=True)
+    rays = []
+    for r in range(1, 32):
+        copy = remote(
+            ray_all_ref.at[here], ray_all_ref.at[here], ray_send.at[r], ray_recv.at[r],
+            cell_peer((here + r) % 32),
+        )
+        copy.start()
+        rays.append(copy)
+
+    image_ref[...] = jnp.zeros_like(image_ref)
+    image_ref[0:nodes, :] = pot_ref[...] * current
+    for a in range(DEG):
+        for y in range(LINES):
+            for s in range(SIDE):
+                start = PLANE * a + LINES * y + DEG * s
+                image_ref[start:start + TILE, :] = (
+                    image_ref[start:start + TILE, :] + value_ref[s, a, TILE * y:TILE * (y + 1), :]
+                )
+    top.wait_recv()
+    image_ref[0:PLANE, :] = image_ref[0:PLANE, :] + under_ref[0:PLANE, :]
+    for copy in rays:
+        copy.wait_recv()
+    total = jnp.sum(ray_all_ref[...], axis=0)
+    rayleigh = total[0:1, :] / (total[1:2, :] + tiny)
+    ray_ref[...] = rayleigh
+    image_ref[0:nodes, :] = current - step_size * (image_ref[0:nodes, :] - rayleigh * current)
+
+    rows = []
+    for r in (6, 2, 5, 3, 7, 1, 4):
+        peer = (me + r) % 8
+        first = pl.multiple_of(peer * ROWS, TILE)
+        copy = remote(
+            image_ref.at[pl.ds(first, ROWS)], rows_ref.at[me], rows_send.at[r], rows_recv.at[r],
+            orb_peer(peer),
+        )
+        copy.start()
+        rows.append(copy)
+    sums = []
+    for r in range(1, 32):
+        copy = remote(
+            sums_ref.at[here], sums_ref.at[here], sums_send.at[r], sums_recv.at[r],
+            cell_peer((here + r) % 32),
+        )
+        copy.start()
+        sums.append(copy)
+    rows_ref[me] = image_ref[pl.ds(pl.multiple_of(me * ROWS, TILE), ROWS), :]
+    for copy in rows + sums:
+        copy.wait_recv()
+    everything = [halo, top] + dens_copies + list(gives.values()) + list(useds.values()) + rays
+    for copy in everything + rows + sums:
+        copy.wait_send()
+
+
+def trial_rows(
+    orbitals, occupations, external, core_density, cell_scale, stiffness,
+    touched_atom, touched_cells, projectors, coupling, collective_id,
+):
+    nodes = orbitals.shape[0]
+    here = lax.axis_index(CELLS)
+    mine = lax.dynamic_slice_in_dim(touched_atom, here * TOUCH_DEV, TOUCH_DEV)[:, None]
+    column = jnp.arange(10 + 9, dtype=jnp.int32)[None, :]
+    near = (mine - 2 * here + 2 * REACH + 64) % 64
+    hot = (jnp.where(column < 10, near, touched_cells + 10) == column).astype(jnp.float32)
+    scalars = pl.BlockSpec(memory_space=pltpu.SMEM)
+    dma = lambda n: pltpu.SemaphoreType.DMA((n,))
+    vmem = lambda *shape: pltpu.VMEM(shape, jnp.float32)
+    return pl.pallas_call(
+        trial_kernel,
+        out_shape=(
+            jax.ShapeDtypeStruct((8, ROWS, 128), jnp.float32),
+            jax.ShapeDtypeStruct((1, 128), jnp.float32),
+            jax.ShapeDtypeStruct((32, ATOM_DEV, PROJ, 128), jnp.float32),
+        ),
+        in_specs=[scalars] * 2 + [WHOLE] * 7,
+        out_specs=(WHOLE,) * 3,
+        scratch_shapes=[
+            vmem(HALO, 128),
+            vmem(SIDE, EDGE, LINES * TILE, 128),
+            vmem(SIDE, EDGE, LINES * TILE, 128),
+            vmem(8 * ROWS, 128),
+            vmem(HALO, 128),
+            vmem(HALO, 128),
+            vmem(24 * TOUCH_DEV, CELL_NODES),
+            vmem(WINDOW, ATOM_DEV, PROJ, 128),
+            vmem(WINDOW, ATOM_DEV, PROJ, 128),
+            vmem(ATOM_DEV, PROJ, 128),
+            vmem(WINDOW, ATOM_DEV, PROJ, 128),
+            vmem(8, 1, nodes),
+            vmem(32, 2, 128),
+            vmem(nodes, 128),
+            dma(2), dma(8), dma(8), dma(5), dma(5), dma(5), dma(5),
+            dma(2), dma(32), dma(32), dma(8), dma(8), dma(32), dma(32),
+        ],
+        compiler_params=pltpu.CompilerParams(
+            collective_id=collective_id, has_side_effects=True, vmem_limit_bytes=48 * 1024 * 1024
+        ),
+    )(
+        cell_scale, hot, orbitals, occupations.reshape(1, -1),
+        external.reshape(1, -1), core_density.reshape(1, -1), stiffness, projectors, coupling,
+    )
+
+
+def owned_kernel(owner_ref, sums_ref, out_ref):
+    here = lax.axis_index("xl") * 16 + lax.axis_index("z") * 2 + lax.axis_index("core")
+    out_ref[...] = jnp.zeros_like(out_ref)
+
+    def place(atom, count):
+        held = owner_ref[atom, 0] == here
+
+        @pl.when(held)
+        def _():
+            out_ref[jnp.minimum(count, OWN_CAP - 1)] = sums_ref[atom // ATOM_DEV, atom % ATOM_DEV]
+
+        return count + jnp.where(held, 1, 0)
+
+    lax.fori_loop(0, owner_ref.shape[0], place, 0)
+
+
+def owned_rows(sums, atom_owner):
+    return pl.pallas_call(
+        owned_kernel,
+        out_shape=jax.ShapeDtypeStruct((OWN_CAP, PROJ, 128), jnp.float32),
+        in_specs=[pl.BlockSpec(memory_space=pltpu.SMEM), WHOLE],
+        out_specs=WHOLE,
+    )(atom_owner, sums)
 
 
 def per_device(
@@ -434,69 +718,16 @@
     coupling,
     atom_owner,
 ):
-    n_cells = lax.axis_size(CELLS)
-    node_dev, width = orbitals.shape
-    total_nodes = node_dev * n_cells
-    layers = THICK * DEG
-    side_nodes = SIDE * DEG + 1
-    here = lax.axis_index(CELLS)
-    proj_count = projectors.shape[2]
-    atom_count = atom_owner.shape[0]
-    owner = atom_owner[:, 0]
-    atom_index = jnp.arange(atom_count, dtype=jnp.int32)
-    earlier = (owner[None, :] == owner[:, None]) & (atom_index[None, :] < atom_index[:, None])
-    owner_rank = jnp.sum(earlier.astype(jnp.int32), axis=1)
-    own_slot = owner * OWN_CAP + owner_rank
-    slot_all = jnp.sum(
-        jnp.where(touched_atom[:, None] == atom_index[None, :], own_slot[None, :], 0), axis=1
-    )
-    my_slots = here * OWN_CAP + jnp.arange(OWN_CAP, dtype=jnp.int32)
-    owned_hot = (slot_all[None, :] == my_slots[:, None]).astype(jnp.float32)
-    flat_coupling = coupling.reshape(atom_count, proj_count * proj_count)
-    mine = lax.dynamic_slice_in_dim(touched_atom, here * TOUCH_DEV, TOUCH_DEV)
-    pair_hot = (mine[:, None] == touched_atom[None, :]).astype(jnp.float32)
-    mine_pick = (mine[:, None] == atom_index[None, :]).astype(jnp.float32)
-    mine_coupling = jnp.dot(mine_pick, flat_coupling, precision=highest).reshape(
-        TOUCH_DEV, proj_count, proj_count
-    )
-    cell_hot = (
-        touched_cells[:, :, None] == jnp.arange(CELL_DEV, dtype=jnp.int32)[None, None, :]
-    ).astype(jnp.float32)
-    spread = jnp.einsum("tqc,tqpn->tpcn", cell_hot, projectors, precision=highest).reshape(
-        TOUCH_DEV * proj_count, CELL_DEV * CELL_NODES
-    )
-    current = orbitals
-    partial_density = jnp.dot(current * current, occupations, precision=highest)
-    density = over_copies(partial_density, ORBS)
-    potential = external - exchange_coef * jnp.cbrt(density + core_density)
-    grid = current.reshape(layers, side_nodes, side_nodes, width)
-    upper_layer = passed_along(grid[0], CELLS, -1)
-    cells = cut_cells(grid, upper_layer)
-    local = cell_scale[:, None, None] * jnp.einsum(
-        "mn,cnr->cmr", stiffness, cells, precision=highest
-    )
-    contrib = jnp.dot(
-        spread, cells.reshape(CELL_DEV * CELL_NODES, width), precision=highest
-    ).reshape(TOUCH_DEV, proj_count, width)
-    piece = gather_axes(contrib, (("xl", "z"), "core"), 0)
-    owned = jnp.einsum("kt,tpr->kpr", owned_hot, piece, precision=highest)
-    touched_sums = jnp.einsum("kt,tpr->kpr", pair_hot, piece, precision=highest)
-    returned = jnp.einsum("tpq,tqr->tpr", mine_coupling, touched_sums, precision=highest)
-    nonlocal_term = jnp.einsum(
-        "kn,kr->nr", spread, returned.reshape(TOUCH_DEV * proj_count, width), precision=highest
-    ).reshape(CELL_DEV, CELL_NODES, width)
-    lower, upper = add_cells(local + nonlocal_term, layers)
-    lower = lower.at[DEG::DEG].add(upper[:-1])
-    carried = passed_along(upper[-1], CELLS, 1)
-    lower = lower.at[0].add(carried)
-    image = lower.reshape(node_dev, width) + potential[:, None] * current
-    numerator, denominator = packed_total(
-        (jnp.sum(current * image, axis=0), jnp.sum(current * current, axis=0)), CELLS
-    )
-    rayleigh = numerator / (denominator + tiny)
-    trial = current - step_size * (image - rayleigh[None, :] * current)
-    current = orthonormal(trial, total_nodes)
-    return (current, rayleigh, owned)
+    nodes = orbitals.shape[0]
+    rows, rayleigh, sums = trial_rows(
+        orbitals, occupations, external, core_density, cell_scale, stiffness,
+        touched_atom, touched_cells, projectors, coupling, 1,
+    )
+    blocks = total_blocks(gram(rows), 2)
+    solved = solve_rows(blocks, rows, 1.0 / (nodes * 32))
+    back = exchange_rows(solved, 3)
+    current = back.reshape(8 * ROWS, 128)[:nodes]
+    return (current, rayleigh.reshape(-1), owned_rows(sums, atom_owner))
 
 
 def solution(mesh):

time: 397 us -> 189 us (0.48)
  local copies, waits for them, and re-layouts: 72 us -> 10.8 us
  Pallas kernels: 224 us -> 175 us
  starting transfers between devices: 25.7 us -> 0 us
  waiting for transfers between devices: 22.2 us -> 0 us
  matrix products: 20.5 us -> 0 us
  other arithmetic: 21 us -> 1.59 us
  blocking collectives: 7.99 us -> 0 us
    pallas_call x1, Pallas kernels: 124 us -> 39.4 us  [solve_rows(): pl.pallas_call(functools.partial(solve_kernel, scale), out_shape=jax.Shap...]
    pallas_call x0 -> x2, Pallas kernels: none -> 56.7 us  [the longest x1 53.7 us: trial_rows(): pl.pallas_call(trial_kernel, out_shape=(jax.ShapeDtypeStruct((8, ROWS, 12...]
    all_to_all x3 -> x0, starting transfers between devices: 23.6 us -> none  [from_everyone(): lax.all_to_all(jnp.broadcast_to(value[None], (length, *value.shape)), axi...]
    pallas_call x2 -> x1, Pallas kernels: 41.8 us -> 19.3 us  [exchange_rows(): pl.pallas_call(rows_out_kernel, out_shape=jax.ShapeDtypeStruct((8, ROWS,...]
    all_to_all x3 -> x0, waiting for transfers between devices: 21.7 us -> none  [from_everyone(): lax.all_to_all(jnp.broadcast_to(value[None], (length, *value.shape)), axi...]
    dot_general x8 -> x0, matrix products: 20.5 us -> none  [the longest x1 6.42 us: per_device(): jnp.einsum('kn,kr->nr', spread, returned.reshape(TOUCH_DEV * proj_count,...]
    another operation x24 -> x0, local copies, waits for them, and re-layouts: 18.6 us -> none  [the longest x11 6.65 us: cut_cells(): return jnp.stack(blocks, axis=1).reshape(-1, CELL_NODES, grid.shape[-1])]
    scatter-add x9 -> x0, local copies, waits for them, and re-layouts: 18.3 us -> none  [add_cells(): slabs = slabs.at[:, :, DEG * row_cell:DEG * row_cell + EDGE, DEG * col_ce...]
  transfers between devices with their start and end apart: 5 -> 0, of which waited for: 3 -> 0; matrix products, arithmetic and copies ran while one was open for 9% -> 0% of each run, Pallas kernels for 0% -> 0%
where the time goes in v2:
time: 189 us; the launch traced here: 188 us
  Pallas kernels  175 us (93%)
  local copies, waits for them, and re-layouts  10.8 us (6%)
    pallas_call x1, Pallas kernels, total_blocks(): pl.pallas_call(total_kernel, out_shape=jax.ShapeDtypeStruct(pieces.shape,...  55.1 us
    pallas_call x1, Pallas kernels, trial_rows(): pl.pallas_call(trial_kernel, out_shape=(jax.ShapeDtypeStruct((8, ROWS, 12...  53.7 us
    pallas_call x1, Pallas kernels, solve_rows(): pl.pallas_call(functools.partial(solve_kernel, scale), out_shape=jax.Shap...  39.4 us
    pallas_call x1, Pallas kernels, exchange_rows(): pl.pallas_call(rows_out_kernel, out_shape=jax.ShapeDtypeStruct((8, ROWS,...  19.3 us
    unnamed x16, local copies, waits for them, and re-layouts  7.02 us
    pallas_call x1, Pallas kernels, gram(): pl.pallas_call(gram_kernel, out_shape=jax.ShapeDtypeStruct((36, 128, 128)...  4.84 us

profile of v2, /device:TPU:1, one launch (start us, length us, event | category | flops | bytes accessed | tf_op | source)
XLA Modules:
  0.0 188.4 jit_solution(11917678555794036452)
XLA Ops:
  0.6 0.0 copy-start.4
  0.6 0.0 copy-start.5
  0.7 0.0 copy-start.1
  0.7 0.9 and_select_fusion
  1.5 0.7 add_bitcast_fusion
  2.2 0.1 fusion.hot_ref
  2.3 0.7 reshape.42.ext_ref
  3.0 0.7 reshape.43.core_ref
  3.7 1.4 copy.16.owner_ref
  5.0 0.9 copy.14.proj_ref
  6.0 1.3 copy.15.coup_ref
  7.3 0.0 copy-done.4
  7.3 0.0 copy-done.5
  7.3 0.0 copy-done.1
  7.3 0.0 copy-start.3
  7.3 1.0 copy-done.3
  8.3 53.7 %shard_map.130 = (f32[8,272,128]{2,1,0:T(8,128)S(1)}, f32[1,128]{1,0:T(1,128)S(1)}, f32[32,2,18,128]{3,2,1,0:T(8,128)S(1)}) custom-call(f32[9]{0:T(128)S(1)} %copy-done.4, f32[6,19]{1,0:T(8,128)S(1)} %fusion.hot_ref, f32[2166,128]{1,0:T(8,128)S(1)} %copy-done.1, f32[1,128]{1,0:T(1,128)S(1)} %bitcast.7, f32[1,2166]{1,0:T(1,128)S(1)} %reshape.42.ext_ref, ...), custom_call_target="tpu_custom_call" | custom-call | tf_op jit(solution)/shard_map/pallas_call | solution.py:647
  62.0 0.0 copy-start
  62.0 1.0 copy-done
  63.1 0.0 copy-start.2
  63.1 0.9 copy-done.2
  63.9 3.0 %shard_map.135 = f32[5,18,128]{2,1,0:T(8,128)} custom-call(s32[64,1]{1,0:T(8,128)} %copy.16.owner_ref, f32[32,2,18,128]{3,2,1,0:T(8,128)} %copy-done.2), custom_call_target="tpu_custom_call" | custom-call | tf_op jit(solution)/shard_map/pallas_call | solution.py:700
  66.9 4.8 %shard_map.131 = f32[36,128,128]{2,1,0:T(8,128)} custom-call(f32[8,272,128]{2,1,0:T(8,128)} %copy-done), custom_call_target="tpu_custom_call" | custom-call | tf_op jit(solution)/shard_map/pallas_call | solution.py:118
  71.8 55.1 %shard_map.132 = f32[2,8,288,128]{3,2,1,0:T(8,128)} custom-call(f32[2,8,288,128]{3,2,1,0:T(8,128)} %bitcast.10), custom_call_target="tpu_custom_call" | custom-call | tf_op jit(solution)/shard_map/pallas_call | solution.py:217
  126.9 39.4 %shard_map.133.t_ref = f32[8,272,128]{2,1,0:T(8,128)} custom-call(f32[36,128,128]{2,1,0:T(8,128)} %bitcast.9, f32[8,272,128]{2,1,0:T(8,128)} %copy-done), custom_call_target="tpu_custom_call" | custom-call | tf_op jit(solution)/shard_map/pallas_call | solution.py:346
  166.2 19.3 %shard_map.134 = f32[8,272,128]{2,1,0:T(8,128)} custom-call(f32[8,272,128]{2,1,0:T(8,128)} %shard_map.133.t_ref), custom_call_target="tpu_custom_call" | custom-call | tf_op jit(solution)/shard_map/pallas_call | solution.py:88
  185.6 2.3 %slice.4 = f32[2166,128]{1,0:T(8,128)} slice(f32[2176,128]{1,0:T(8,128)} %bitcast.11), slice={[0:2166], [0:128]} | slice | bytes 2217984 | tf_op jit(solution)/shard_map/slice | solution.py:729
  187.9 0.5 copy.18
  (1 shorter events, 0.0 us)
Async XLA Ops:
  0.6 6.6 %copy-start.4 = (f32[9]{0:T(128)S(1)}, f32[9]{0:T(128)}, u32[]{:S(2)}) copy-start(f32[9]{0:T(128)} %scale_ref.1) | copy-start | bytes 112
  0.6 6.6 %copy-start.5 = (f32[128]{0:T(128)S(1)}, f32[128]{0:T(128)}, u32[]{:S(2)}) copy-start(f32[128]{0:T(128)} %param.12) | copy-start | bytes 1540
  0.7 6.6 %copy-start.1 = (f32[2166,128]{1,0:T(8,128)S(1)}, f32[2166,128]{1,0:T(8,128)}, u32[]{:S(2)}) copy-start(f32[2166,128]{1,0:T(8,128)} %c_ref.1) | copy-start | bytes 3326980
  7.3 1.0 copy-start.3
  62.0 1.0 copy-start
  63.1 0.9 copy-start.2

commit v3 on v2

--- a/solution.py
+++ b/solution.py
@@ -70,32 +70,41 @@
     )
 
 
-def rows_out_kernel(t_ref, out_ref, send, recv):
+def rows_back_kernel(t_ref, out_ref, full_ref, send, recv, own):
     me = my_orb()
     greet([orb_peer((me + r) % 8) for r in range(1, 8)])
+    mine = pl.ds(pl.multiple_of(me * ROWS, 8), ROWS)
     copies = []
     for r in (6, 2, 5, 3, 7, 1, 4):
         peer = (me + r) % 8
-        copy = remote(t_ref.at[peer], out_ref.at[me], send.at[r], recv.at[r], orb_peer(peer))
+        copy = remote(t_ref.at[peer], full_ref.at[mine], send.at[r], recv.at[r], orb_peer(peer))
         copy.start()
         copies.append(copy)
-    out_ref[me] = t_ref[me]
+    local = pltpu.make_async_copy(t_ref.at[me], full_ref.at[mine], own)
+    local.start()
+    local.wait()
     for copy in copies:
         copy.wait()
-
-
-def exchange_rows(value, collective_id):
+    out_ref[...] = full_ref[0:out_ref.shape[0], :]
+
+
+def rows_back(value, nodes, collective_id):
     return pl.pallas_call(
-        rows_out_kernel,
-        out_shape=jax.ShapeDtypeStruct((8, ROWS, 128), jnp.float32),
-        in_specs=[WHOLE],
+        rows_back_kernel,
+        out_shape=jax.ShapeDtypeStruct((nodes, 128), jnp.float32),
+        in_specs=[pl.BlockSpec(memory_space=pltpu.HBM)],
         out_specs=WHOLE,
-        scratch_shapes=[pltpu.SemaphoreType.DMA((8,)), pltpu.SemaphoreType.DMA((8,))],
-        compiler_params=pltpu.CompilerParams(collective_id=collective_id, has_side_effects=True),
+        scratch_shapes=[
+            pltpu.VMEM((8 * ROWS, 128), jnp.float32),
+            pltpu.SemaphoreType.DMA((8,)), pltpu.SemaphoreType.DMA((8,)), pltpu.SemaphoreType.DMA,
+        ],
+        compiler_params=pltpu.CompilerParams(
+            collective_id=collective_id, has_side_effects=True, vmem_limit_bytes=62 * 1024 * 1024
+        ),
     )(value)
 
 
-def gram_kernel(x_ref, out_ref, left_ref, right_ref):
+def gram(x_ref, out_ref, left_ref, right_ref):
     for j in range(8):
         high, low = split(x_ref[j])
         lanes = pl.ds(128 * j, 128)
@@ -111,20 +120,11 @@
             (((0,), (0,)), ((), ())), preferred_element_type=jnp.float32,
         )
         for j in range(i + 1):
-            out_ref[i * (i + 1) // 2 + j] = product[:, 128 * j:128 * (j + 1)]
-
-
-def gram(rows):
-    return pl.pallas_call(
-        gram_kernel,
-        out_shape=jax.ShapeDtypeStruct((36, 128, 128), jnp.float32),
-        in_specs=[WHOLE],
-        out_specs=WHOLE,
-        scratch_shapes=[pltpu.VMEM((3 * ROWS, 1024), jnp.bfloat16)] * 2,
-    )(rows)
-
-
-def total_kernel(
+            block = i * (i + 1) // 2 + j
+            out_ref[128 * block:128 * (block + 1), :] = product[:, 128 * j:128 * (j + 1)]
+
+
+def total_over_all(
     m_ref, out_ref, pair_ref, mine_ref, orb_ref, sum_ref, cut_ref, site_ref, done_ref,
     pair_send, pair_recv, orb_send, orb_recv, site_send, site_recv,
     back_send, back_recv, home_send, home_recv, last_send, last_recv,
@@ -134,17 +134,16 @@
     here = my_site()
     partner = {"core": 1 - core}
     order = (6, 2, 5, 3, 7, 1, 4)
-    greet(
-        [partner]
-        + [orb_peer((me + r) % 8) for r in range(1, 8)]
-        + [site_peer((here + r) % 16) for r in range(1, 16)]
-    )
+
+    def part(half, piece):
+        return pl.ds(pl.multiple_of((8 * half + piece) * PIECE, 8), PIECE)
+
     pending = []
     arrivals = {}
     for r in order + (0,):
         piece = (me + r) % 8
         copy = remote(
-            m_ref.at[1 - core, piece], pair_ref.at[piece], pair_send.at[r], pair_recv.at[r], partner
+            m_ref.at[part(1 - core, piece)], pair_ref.at[piece], pair_send.at[r], pair_recv.at[r], partner
         )
         copy.start()
         arrivals[r] = copy
@@ -153,7 +152,7 @@
     for r in order + (0,):
         piece = (me + r) % 8
         arrivals[r].wait_recv()
-        mine_ref[piece] = m_ref[core, piece] + pair_ref[piece]
+        mine_ref[piece] = m_ref[part(core, piece), :] + pair_ref[piece]
         if r:
             copy = remote(mine_ref.at[piece], orb_ref.at[r], orb_send.at[r], orb_recv.at[r], orb_peer(piece))
             copy.start()
@@ -182,8 +181,6 @@
         copy = remote(done_ref.at[here], done_ref.at[here], back_send.at[r], back_recv.at[r], site_peer(peer))
         copy.start()
         thirds.append(copy)
-    for copy in seconds:
-        copy.wait_send()
     for copy in thirds:
         copy.wait_recv()
     for i in range(16):
@@ -204,35 +201,9 @@
         forward = remote(place, place, last_send.at[r], last_recv.at[r], partner)
         forward.start()
         lasts.append(forward)
-    for copy in pending + firsts + thirds + fourths + lasts:
-        copy.wait_send()
     for copy in lasts:
         copy.wait_recv()
-
-
-def total_blocks(blocks, collective_id):
-    pieces = blocks.reshape(2, 8, PIECE, 128)
-    eight = pltpu.SemaphoreType.DMA((8,))
-    sixteen = pltpu.SemaphoreType.DMA((16,))
-    total = pl.pallas_call(
-        total_kernel,
-        out_shape=jax.ShapeDtypeStruct(pieces.shape, jnp.float32),
-        in_specs=[WHOLE],
-        out_specs=WHOLE,
-        scratch_shapes=[
-            pltpu.VMEM((8, PIECE, 128), jnp.float32),
-            pltpu.VMEM((8, PIECE, 128), jnp.float32),
-            pltpu.VMEM((8, PIECE, 128), jnp.float32),
-            pltpu.VMEM((PIECE, 128), jnp.float32),
-            pltpu.VMEM((16, SLOT, 128), jnp.float32),
-            pltpu.VMEM((16, SLOT, 128), jnp.float32),
-            pltpu.VMEM((16, SLOT, 128), jnp.float32),
-            eight, eight, eight, eight, sixteen, sixteen,
-            sixteen, sixteen, eight, eight, eight, eight,
-        ],
-        compiler_params=pltpu.CompilerParams(collective_id=collective_id, has_side_effects=True),
-    )(pieces)
-    return total.reshape(36, 128, 128)
+    return pending + firsts + seconds + thirds + fourths + lasts
 
 
 def product(x, y):
@@ -262,7 +233,28 @@
     return jnp.concatenate(split(x), axis=1)
 
 
-def solve_kernel(scale, m_ref, t_ref, out_ref, panel_ref, left_ref, inv_ref, work_ref, unit_ref):
+def place_owned(owner_ref, sums_ref, owned_ref):
+    here = lax.axis_index("xl") * 16 + lax.axis_index("z") * 2 + lax.axis_index("core")
+    owned_ref[...] = jnp.zeros_like(owned_ref)
+
+    def place(atom, count):
+        held = owner_ref[atom] == here
+
+        @pl.when(held)
+        def _():
+            owned_ref[jnp.minimum(count, OWN_CAP - 1)] = sums_ref[atom // ATOM_DEV, atom % ATOM_DEV]
+
+        return count + jnp.where(held, 1, 0)
+
+    lax.fori_loop(0, owner_ref.shape[0], place, 0)
+
+
+def solve_kernel(
+    scale, owner_ref, m_ref, t_ref, sums_ref, ray_ref, out_ref, owned_ref, rayleigh_ref,
+    panel_ref, left_ref, inv_ref, work_ref, unit_ref,
+):
+    rayleigh_ref[...] = ray_ref[...]
+    place_owned(owner_ref, sums_ref, owned_ref)
     row = lax.broadcasted_iota(jnp.int32, (128, 128), 0)
     col = lax.broadcasted_iota(jnp.int32, (128, 128), 1)
     eye = (row == col).astype(jnp.float32)
@@ -342,12 +334,16 @@
                 )
 
 
-def solve_rows(blocks, rows, scale):
+def solve_rows(blocks, rows, scale, atom_owner, sums, rayleigh):
     return pl.pallas_call(
         functools.partial(solve_kernel, scale),
-        out_shape=jax.ShapeDtypeStruct((8, ROWS, 128), jnp.float32),
-        in_specs=[WHOLE, WHOLE],
-        out_specs=WHOLE,
+        out_shape=(
+            jax.ShapeDtypeStruct((8, ROWS, 128), jnp.float32),
+            jax.ShapeDtypeStruct((OWN_CAP, PROJ, 128), jnp.float32),
+            jax.ShapeDtypeStruct((1, 128), jnp.float32),
+        ),
+        in_specs=[pl.BlockSpec(memory_space=pltpu.SMEM)] + [WHOLE] * 4,
+        out_specs=(WHOLE,) * 3,
         scratch_shapes=[
             pltpu.VMEM((8, 1024 + ROWS, 128), jnp.float32),
             pltpu.VMEM((1024 + ROWS, 256), jnp.bfloat16),
@@ -355,7 +351,8 @@
             pltpu.VMEM((128, 128), jnp.float32),
             pltpu.VMEM((128, 128), jnp.float32),
         ],
-    )(blocks, rows)
+        compiler_params=pltpu.CompilerParams(vmem_limit_bytes=62 * 1024 * 1024),
+    )(atom_owner, blocks, rows, sums, rayleigh)
 
 
 WINDOW = 2 * REACH + 1
@@ -388,12 +385,14 @@
 
 def trial_kernel(
     scale_ref, hot_ref,
-    c_ref, occ_ref, ext_ref, core_ref, stiff_ref, proj_ref, coup_ref,
-    rows_ref, ray_ref, sums_ref,
+    c_in, occ_in, ext_in, core_in, stiff_in, proj_in, coup_in,
+    rows_ref, ray_ref, sums_ref, total_ref,
+    c_ref, occ_ref, ext_ref, core_ref, stiff_ref, proj_ref, coup_ref, pick_ref, load_sem,
     halo_ref, tile_ref, value_ref, image_ref, top_ref, under_ref, proj24_ref,
     give_ref, take_ref, used_ref, window_ref, dens_ref, ray_all_ref, pot_ref,
     halo_sem, dens_send, dens_recv, give_send, give_recv, used_send, used_recv,
     top_sem, ray_send, ray_recv, rows_send, rows_recv, sums_send, sums_recv,
+    gram_ref, left_ref, right_ref, *total_scratch,
 ):
     nodes = c_ref.shape[0]
     here = lax.axis_index("xl") * 16 + lax.axis_index("z") * 2 + lax.axis_index("core")
@@ -403,14 +402,17 @@
     peers += [orb_peer((me + r) % 8) for r in range(1, 8)]
     for peer in peers:
         pl.semaphore_signal(barrier, inc=1, device_id=peer, device_id_type=MESH_ID)
-    sends = []
-
-    current = c_ref[...]
-    square = current * current
-    occ = occ_ref[...]
-    density = thrice(split(jnp.broadcast_to(occ, (TILE, 128))), split(square), ((1,), (1,)))
-    dens_ref[0] = density[0:1, :]
-
+    loads = [
+        pltpu.make_async_copy(source, target, load_sem.at[i])
+        for i, (source, target) in enumerate(
+            (
+                (stiff_in, stiff_ref), (proj_in, proj_ref), (coup_in, coup_ref), (c_in, c_ref),
+                (occ_in, occ_ref), (ext_in, ext_ref), (core_in, core_ref),
+            )
+        )
+    ]
+    for load in loads:
+        load.start()
     node = lax.broadcasted_iota(jnp.int32, (CELL_NODES, PADDED), 0)
     place = lax.broadcasted_iota(jnp.int32, (CELL_NODES, PADDED), 1)
     inside = (place & 7) < EDGE
@@ -422,13 +424,28 @@
         wide = dot(part, spot, (((1,), (0,)), ((), ()))).astype(jnp.bfloat16)
         return dot(spot, wide, (((0,), (0,)), ((), ()))).astype(jnp.bfloat16)
 
+    loads[0].wait()
     stiff = tuple(both_sides(part) for part in split(stiff_ref[...]))
+    loads[1].wait()
     proj24_ref[...] = jnp.zeros_like(proj24_ref)
     for t in range(TOUCH_DEV):
-        proj24_ref[24 * t:24 * t + PROJ, :] = proj_ref[t, 0]
+        proj24_ref[24 * t:24 * t + PROJ, :] = proj_ref[t, :, 0, :]
     parts = split(proj24_ref[...])
     proj_rows = tuple(dot(p, spot, (((1,), (0,)), ((), ()))).astype(jnp.bfloat16) for p in parts)
     proj_cols = tuple(dot(spot, p, (((0,), (1,)), ((), ()))).astype(jnp.bfloat16) for p in parts)
+
+    loads[2].wait()
+    lane = lax.broadcasted_iota(jnp.int32, (PROJ, 64), 1)
+    for m in range(ATOM_DEV):
+        for p in range(PROJ):
+            column = jnp.sum(jnp.where(lane == 2 * here + m, coup_ref[p], 0.0), axis=1, keepdims=True)
+            pick_ref[m, p] = jnp.broadcast_to(column, (PROJ, 128))
+    for load in loads[3:]:
+        load.wait()
+    current = c_ref[...]
+    square = current * current
+    density = thrice(split(jnp.broadcast_to(occ_ref[...].reshape(1, 128), (TILE, 128))), split(square), ((1,), (1,)))
+    dens_ref[0] = density[0:1, :]
 
     pl.semaphore_wait(barrier, len(peers))
     halo = remote(
@@ -472,12 +489,12 @@
         for t in range(TOUCH_DEV):
             for s in range(SIDE):
                 part = wide[24 * t:24 * t + 24, 128 * s:128 * (s + 1)]
-                contrib[t] = contrib[t] + hot_ref[t, 10 + SIDE * r + s] * part
+                contrib[t] = contrib[t] + hot_ref[10 + SIDE * r + s, t] * part
     for k in range(WINDOW):
         for m in range(ATOM_DEV):
-            total = hot_ref[0, ATOM_DEV * k + m] * contrib[0]
+            total = hot_ref[ATOM_DEV * k + m, 0] * contrib[0]
             for t in range(1, TOUCH_DEV):
-                total = total + hot_ref[t, ATOM_DEV * k + m] * contrib[t]
+                total = total + hot_ref[ATOM_DEV * k + m, t] * contrib[t]
             give_ref[k, m] = total[:PROJ]
     gives = {}
     for k in (0, 4, 1, 3):
@@ -513,7 +530,8 @@
         for k in (0, 1, 3, 4):
             total = total + take_ref[k, m]
         sums_ref[here, m] = total
-        used_ref[m] = thrice(split(coup_ref[2 * here + m]), split(total), ((1,), (0,)))
+        for p in range(PROJ):
+            used_ref[m, p:p + 1, :] = jnp.sum(pick_ref[m, p] * total, axis=0, keepdims=True)
         window_ref[REACH, m] = used_ref[m]
     for q in (0, 4, 1, 3):
         copy = remote(
@@ -528,7 +546,9 @@
     density = dens_ref[0]
     for r in range(1, 8):
         density = density + dens_ref[r]
-    potential = ext_ref[...] - exchange_coef * cube_root(density + core_ref[...])
+    potential = ext_ref[...].reshape(1, nodes) - exchange_coef * cube_root(
+        density + core_ref[...].reshape(1, nodes)
+    )
     pot_ref[...] = dot(
         jnp.broadcast_to(potential, (TILE, nodes)),
         (lax.broadcasted_iota(jnp.int32, (TILE, 128), 0) == 0).astype(jnp.float32),
@@ -542,14 +562,14 @@
         total = jnp.zeros((PROJ, 128), jnp.float32)
         for k in range(WINDOW):
             for m in range(ATOM_DEV):
-                total = total + hot_ref[t, ATOM_DEV * k + m] * window_ref[k, m]
+                total = total + hot_ref[ATOM_DEV * k + m, t] * window_ref[k, m]
         back.append(jnp.concatenate([total, jnp.zeros((24 - PROJ, 128), jnp.float32)], axis=0))
     for r in range(SIDE):
         wide = jnp.concatenate(
             [
                 jnp.concatenate(
                     [
-                        hot_ref[t, 10 + SIDE * r + s] * back[t]
+                        hot_ref[10 + SIDE * r + s, t] * back[t]
                         for t in range(TOUCH_DEV)
                     ],
                     axis=0,
@@ -624,9 +644,13 @@
         copy.start()
         sums.append(copy)
     rows_ref[me] = image_ref[pl.ds(pl.multiple_of(me * ROWS, TILE), ROWS), :]
-    for copy in rows + sums:
-        copy.wait_recv()
-    everything = [halo, top] + dens_copies + list(gives.values()) + list(useds.values()) + rays
+    for copy in rows:
+        copy.wait_recv()
+    gram(rows_ref, gram_ref, left_ref, right_ref)
+    everything = total_over_all(gram_ref, total_ref, *total_scratch)
+    for copy in sums:
+        copy.wait_recv()
+    everything += [halo, top] + dens_copies + list(gives.values()) + list(useds.values()) + rays
     for copy in everything + rows + sums:
         copy.wait_send()
 
@@ -637,10 +661,12 @@
 ):
     nodes = orbitals.shape[0]
     here = lax.axis_index(CELLS)
-    mine = lax.dynamic_slice_in_dim(touched_atom, here * TOUCH_DEV, TOUCH_DEV)[:, None]
-    column = jnp.arange(10 + 9, dtype=jnp.int32)[None, :]
-    near = (mine - 2 * here + 2 * REACH + 64) % 64
-    hot = (jnp.where(column < 10, near, touched_cells + 10) == column).astype(jnp.float32)
+    mine = lax.dynamic_slice_in_dim(touched_atom, here * TOUCH_DEV, TOUCH_DEV)[None, :]
+    line = lax.broadcasted_iota(jnp.int32, (10 + 9, TOUCH_DEV), 0)
+    near = mine - 2 * here + 2 * REACH
+    near = jnp.where(near < 0, near + 64, jnp.where(near >= 64, near - 64, near))
+    cells = touched_cells.reshape(1, -1) + 10
+    hot = jnp.where(jnp.where(line < 10, near, cells) == line, 1.0, 0.0)
     scalars = pl.BlockSpec(memory_space=pltpu.SMEM)
     dma = lambda n: pltpu.SemaphoreType.DMA((n,))
     vmem = lambda *shape: pltpu.VMEM(shape, jnp.float32)
@@ -650,10 +676,14 @@
             jax.ShapeDtypeStruct((8, ROWS, 128), jnp.float32),
             jax.ShapeDtypeStruct((1, 128), jnp.float32),
             jax.ShapeDtypeStruct((32, ATOM_DEV, PROJ, 128), jnp.float32),
+            jax.ShapeDtypeStruct((2, 8, PIECE, 128), jnp.float32),
         ),
-        in_specs=[scalars] * 2 + [WHOLE] * 7,
-        out_specs=(WHOLE,) * 3,
+        in_specs=[scalars] * 2 + [pl.BlockSpec(memory_space=pltpu.HBM)] * 7,
+        out_specs=(WHOLE,) * 4,
         scratch_shapes=[
+            vmem(nodes, 128), vmem(128), vmem(nodes), vmem(nodes), vmem(CELL_NODES, CELL_NODES),
+            vmem(TOUCH_DEV, PROJ, 1, CELL_NODES), vmem(PROJ, PROJ, 64), vmem(ATOM_DEV, PROJ, PROJ, 128),
+            dma(7),
             vmem(HALO, 128),
             vmem(SIDE, EDGE, LINES * TILE, 128),
             vmem(SIDE, EDGE, LINES * TILE, 128),
@@ -670,39 +700,21 @@
             vmem(nodes, 128),
             dma(2), dma(8), dma(8), dma(5), dma(5), dma(5), dma(5),
             dma(2), dma(32), dma(32), dma(8), dma(8), dma(32), dma(32),
+            vmem(16 * PIECE, 128),
+            pltpu.VMEM((3 * ROWS, 1024), jnp.bfloat16),
+            pltpu.VMEM((3 * ROWS, 1024), jnp.bfloat16),
+            vmem(8, PIECE, 128), vmem(8, PIECE, 128), vmem(8, PIECE, 128), vmem(PIECE, 128),
+            vmem(16, SLOT, 128), vmem(16, SLOT, 128), vmem(16, SLOT, 128),
+            dma(8), dma(8), dma(8), dma(8), dma(16), dma(16),
+            dma(16), dma(16), dma(8), dma(8), dma(8), dma(8),
         ],
         compiler_params=pltpu.CompilerParams(
-            collective_id=collective_id, has_side_effects=True, vmem_limit_bytes=48 * 1024 * 1024
+            collective_id=collective_id, has_side_effects=True, vmem_limit_bytes=62 * 1024 * 1024
         ),
     )(
-        cell_scale, hot, orbitals, occupations.reshape(1, -1),
-        external.reshape(1, -1), core_density.reshape(1, -1), stiffness, projectors, coupling,
-    )
-
-
-def owned_kernel(owner_ref, sums_ref, out_ref):
-    here = lax.axis_index("xl") * 16 + lax.axis_index("z") * 2 + lax.axis_index("core")
-    out_ref[...] = jnp.zeros_like(out_ref)
-
-    def place(atom, count):
-        held = owner_ref[atom, 0] == here
-
-        @pl.when(held)
-        def _():
-            out_ref[jnp.minimum(count, OWN_CAP - 1)] = sums_ref[atom // ATOM_DEV, atom % ATOM_DEV]
-
-        return count + jnp.where(held, 1, 0)
-
-    lax.fori_loop(0, owner_ref.shape[0], place, 0)
-
-
-def owned_rows(sums, atom_owner):
-    return pl.pallas_call(
-        owned_kernel,
-        out_shape=jax.ShapeDtypeStruct((OWN_CAP, PROJ, 128), jnp.float32),
-        in_specs=[pl.BlockSpec(memory_space=pltpu.SMEM), WHOLE],
-        out_specs=WHOLE,
-    )(atom_owner, sums)
+        cell_scale, hot, orbitals, occupations,
+        external, core_density, stiffness, projectors.transpose(0, 2, 1, 3), coupling.transpose(1, 2, 0),
+    )
 
 
 def per_device(
@@ -719,15 +731,14 @@
     atom_owner,
 ):
     nodes = orbitals.shape[0]
-    rows, rayleigh, sums = trial_rows(
+    rows, rayleigh, sums, blocks = trial_rows(
         orbitals, occupations, external, core_density, cell_scale, stiffness,
         touched_atom, touched_cells, projectors, coupling, 1,
     )
-    blocks = total_blocks(gram(rows), 2)
-    solved = solve_rows(blocks, rows, 1.0 / (nodes * 32))
-    back = exchange_rows(solved, 3)
-    current = back.reshape(8 * ROWS, 128)[:nodes]
-    return (current, rayleigh.reshape(-1), owned_rows(sums, atom_owner))
+    solved, owned, rayleigh = solve_rows(
+        blocks.reshape(36, 128, 128), rows, 1.0 / (nodes * 32), atom_owner.reshape(-1), sums, rayleigh
+    )
+    return (rows_back(solved, nodes, 2), rayleigh.reshape(-1), owned)
 
 
 def solution(mesh):

time: 189 us -> 174 us (0.921)
  local copies, waits for them, and re-layouts: 10.8 us -> 2.31 us
  Pallas kernels: 175 us -> 168 us
    pallas_call x5 -> x2, Pallas kernels: 122 us -> 58.6 us  [the longest x1 40.5 us: solve_rows(): pl.pallas_call(functools.partial(solve_kernel, scale), out_shape=(jax.Sha...]
    pallas_call x1, Pallas kernels: 53.7 us -> 110 us  [trial_rows(): pl.pallas_call(trial_kernel, out_shape=(jax.ShapeDtypeStruct((8, ROWS, 12...]
    unnamed x16 -> x1, local copies, waits for them, and re-layouts: 7.02 us -> 2.31 us
    slice x1 -> x0, local copies, waits for them, and re-layouts: 2.31 us -> none  [per_device(): current = back.reshape(8 * ROWS, 128)[:nodes]]
where the time goes in v3:
time: 174 us; the launch traced here: 173 us
  Pallas kernels  168 us (97%)
  local copies, waits for them, and re-layouts  2.31 us (1%)
  other arithmetic  2.1 us (1%)
    pallas_call x1, Pallas kernels, trial_rows(): pl.pallas_call(trial_kernel, out_shape=(jax.ShapeDtypeStruct((8, ROWS, 12...  110 us
    pallas_call x1, Pallas kernels, solve_rows(): pl.pallas_call(functools.partial(solve_kernel, scale), out_shape=(jax.Sha...  40.5 us
    pallas_call x1, Pallas kernels, rows_back(): pl.pallas_call(rows_back_kernel, out_shape=jax.ShapeDtypeStruct((nodes, 1...  18.1 us

profile of v3, /device:TPU:1, one launch (start us, length us, event | category | flops | bytes accessed | tf_op | source)
XLA Modules:
  0.0 173.2 jit_solution(1890415764744468035)
XLA Ops:
  0.6 0.8 compare_select_fusion.1
  1.4 0.7 add_bitcast_fusion
  2.1 0.7 fusion.hot_ref
  2.7 109.6 %shard_map.130 = (f32[8,272,128]{2,1,0:T(8,128)}, f32[1,128]{1,0:T(1,128)}, f32[32,2,18,128]{3,2,1,0:T(8,128)}, f32[2,8,288,128]{3,2,1,0:T(8,128)}) custom-call(f32[9]{0:T(128)} %scale_ref.1, f32[19,6]{1,0:T(8,128)} %fusion.hot_ref, f32[2166,128]{1,0:T(8,128)} %c_in.1, f32[128]{0:T(128)} %occ_in.1, f32[2166]{0:T(1024)} %ext_in.1, f32[2166]{0:T(1024)} %core_in.1, ...), custom_call_target="tpu_custom_call" | custom-call | tf_op jit(solution)/shard_map/pallas_call | solution.py:673
  112.3 40.5 %shard_map.131 = (f32[8,272,128]{2,1,0:T(8,128)}, f32[5,18,128]{2,1,0:T(8,128)}, f32[1,128]{1,0:T(1,128)}) custom-call(s32[64]{0:T(128)} %bitcast.10, f32[36,128,128]{2,1,0:T(8,128)} %bitcast.7, f32[8,272,128]{2,1,0:T(8,128)} %get-tuple-element.11.t_ref, f32[32,2,18,128]{3,2,1,0:T(8,128)} %get-tuple-element.12.sums_ref, f32[1,128]{1,0:T(1,128)} %get-tuple-element.13.ray_ref), custom_call_target="tpu_custom_call" | custom-call | tf_op jit(solution)/shard_map/pallas_call | solution.py:338
  152.8 18.1 %shard_map.132 = f32[2166,128]{1,0:T(8,128)} custom-call(f32[8,272,128]{2,1,0:T(8,128)} %get-tuple-element.14.t_ref), custom_call_target="tpu_custom_call" | custom-call | tf_op jit(solution)/shard_map/pallas_call | solution.py:92
  170.9 2.3 %copy.15 = f32[2166,128]{1,0:T(8,128)} copy(f32[2166,128]{1,0:T(8,128)} %shard_map.132) | data formatting | bytes 2217984
  (1 shorter events, 0.0 us)

commit v4 on v3

--- a/solution.py
+++ b/solution.py
@@ -28,8 +28,11 @@
 
 
 ROWS = 272
-PIECE = 288
-SLOT = 18
+EDGE_ROWS = 48
+BODY_ROWS = 224
+FORTH = 1536
+ORB_PIECE, ORB_SLOT = 192, 12
+SITE_PIECE, SITE_SLOT = 48, 6
 MESH_ID = pl.DeviceIdType.MESH
 WHOLE = pl.BlockSpec(memory_space=pltpu.VMEM)
 
@@ -70,20 +73,29 @@
     )
 
 
-def rows_back_kernel(t_ref, out_ref, full_ref, send, recv, own):
+def rows_back_kernel(t_ref, out_ref, full_ref, edge_sem, body_sem, own):
     me = my_orb()
     greet([orb_peer((me + r) % 8) for r in range(1, 8)])
-    mine = pl.ds(pl.multiple_of(me * ROWS, 8), ROWS)
+    edge = pl.ds(pl.multiple_of(EDGE_ROWS * me, 8), EDGE_ROWS)
+    body = pl.ds(pl.multiple_of(8 * EDGE_ROWS + BODY_ROWS * me, 8), BODY_ROWS)
     copies = []
     for r in (6, 2, 5, 3, 7, 1, 4):
         peer = (me + r) % 8
-        copy = remote(t_ref.at[peer], full_ref.at[mine], send.at[r], recv.at[r], orb_peer(peer))
-        copy.start()
-        copies.append(copy)
-    local = pltpu.make_async_copy(t_ref.at[me], full_ref.at[mine], own)
-    local.start()
-    local.wait()
-    for copy in copies:
+        for source, target, sems in (
+            (pl.ds(EDGE_ROWS, BODY_ROWS), body, body_sem), (pl.ds(0, EDGE_ROWS), edge, edge_sem)
+        ):
+            copy = remote(
+                t_ref.at[peer, source], full_ref.at[target], sems.at[0, r], sems.at[1, r], orb_peer(peer)
+            )
+            copy.start()
+            copies.append(copy)
+    locals_ = [
+        pltpu.make_async_copy(t_ref.at[me, pl.ds(EDGE_ROWS, BODY_ROWS)], full_ref.at[body], own.at[0]),
+        pltpu.make_async_copy(t_ref.at[me, pl.ds(0, EDGE_ROWS)], full_ref.at[edge], own.at[1]),
+    ]
+    for copy in locals_:
+        copy.start()
+    for copy in locals_ + copies:
         copy.wait()
     out_ref[...] = full_ref[0:out_ref.shape[0], :]
 
@@ -96,10 +108,10 @@
         out_specs=WHOLE,
         scratch_shapes=[
             pltpu.VMEM((8 * ROWS, 128), jnp.float32),
-            pltpu.SemaphoreType.DMA((8,)), pltpu.SemaphoreType.DMA((8,)), pltpu.SemaphoreType.DMA,
+            pltpu.SemaphoreType.DMA((2, 8)), pltpu.SemaphoreType.DMA((2, 8)), pltpu.SemaphoreType.DMA((2,)),
         ],
         compiler_params=pltpu.CompilerParams(
-            collective_id=collective_id, has_side_effects=True, vmem_limit_bytes=62 * 1024 * 1024
+            collective_id=collective_id, has_side_effects=True, vmem_limit_bytes=58 * 1024 * 1024
         ),
     )(value)
 
@@ -125,85 +137,131 @@
 
 
 def total_over_all(
-    m_ref, out_ref, pair_ref, mine_ref, orb_ref, sum_ref, cut_ref, site_ref, done_ref,
-    pair_send, pair_recv, orb_send, orb_recv, site_send, site_recv,
-    back_send, back_recv, home_send, home_recv, last_send, last_recv,
+    m_ref, out_ref, pair_ref, mine_ref,
+    orb_ref, sum_ref, cut_ref, site_ref, done_ref,
+    orb2_ref, sum2_ref, cut2_ref, site2_ref, done2_ref,
+    pair_sem, orb_sem, site_sem, back_sem, home_sem, last_sem,
+    orb2_sem, site2_sem, back2_sem, home2_sem, last2_sem,
 ):
     core = lax.axis_index("core")
     me = my_orb()
     here = my_site()
     partner = {"core": 1 - core}
     order = (6, 2, 5, 3, 7, 1, 4)
-
-    def part(half, piece):
-        return pl.ds(pl.multiple_of((8 * half + piece) * PIECE, 8), PIECE)
-
-    pending = []
+    sites = (4, 12, 5, 3, 13, 11, 6, 2, 14, 10, 7, 1, 15, 9, 8)
+    half = m_ref.shape[0] // 2
+    every = []
+
+    def rows(start, size, base=0):
+        return pl.ds(pl.multiple_of(base + start, 8), size)
+
+    def go(source, target, sems, index, peer):
+        copy = remote(source, target, sems.at[0, index], sems.at[1, index], peer)
+        copy.start()
+        every.append(copy)
+        return copy
+
+    mine_base = core * half
+    other_base = (1 - core) * half
+    first = go(
+        m_ref.at[rows(FORTH, half - FORTH, other_base)], pair_ref.at[pl.ds(FORTH, half - FORTH)],
+        pair_sem, 8, partner,
+    )
     arrivals = {}
     for r in order + (0,):
-        piece = (me + r) % 8
-        copy = remote(
-            m_ref.at[part(1 - core, piece)], pair_ref.at[piece], pair_send.at[r], pair_recv.at[r], partner
-        )
-        copy.start()
-        arrivals[r] = copy
-        pending.append(copy)
-    firsts = []
+        start = ORB_PIECE * ((me + r) % 8)
+        arrivals[r] = go(
+            m_ref.at[rows(start, ORB_PIECE, other_base)], pair_ref.at[rows(start, ORB_PIECE)],
+            pair_sem, r, partner,
+        )
+    first.wait_recv()
+    mine_ref[FORTH:half, :] = m_ref[rows(FORTH, half - FORTH, mine_base), :] + pair_ref[FORTH:half, :]
+    spread2 = {}
+    for r in sites:
+        peer = (here + r) % 16
+        spread2[r] = go(
+            mine_ref.at[rows(SITE_PIECE * peer, SITE_PIECE, FORTH)], site2_ref.at[r], site2_sem, r,
+            site_peer(peer),
+        )
+    spread1 = {}
     for r in order + (0,):
-        piece = (me + r) % 8
+        peer = (me + r) % 8
+        start = ORB_PIECE * peer
         arrivals[r].wait_recv()
-        mine_ref[piece] = m_ref[part(core, piece), :] + pair_ref[piece]
+        mine_ref[rows(start, ORB_PIECE), :] = (
+            m_ref[rows(start, ORB_PIECE, mine_base), :] + pair_ref[rows(start, ORB_PIECE), :]
+        )
         if r:
-            copy = remote(mine_ref.at[piece], orb_ref.at[r], orb_send.at[r], orb_recv.at[r], orb_peer(piece))
-            copy.start()
-            firsts.append(copy)
-    total = mine_ref[me]
-    for copy, r in zip(firsts, order):
-        copy.wait_recv()
+            spread1[r] = go(
+                mine_ref.at[rows(start, ORB_PIECE)], orb_ref.at[r], orb_sem, r, orb_peer(peer)
+            )
+    total = mine_ref[rows(SITE_PIECE * here, SITE_PIECE, FORTH), :]
+    for r in sites:
+        spread2[r].wait_recv()
+        total = total + site2_ref[r]
+    sum2_ref[...] = total
+    for i in range(8):
+        cut2_ref[i] = sum2_ref[SITE_SLOT * i:SITE_SLOT * (i + 1), :]
+    inner2 = {}
+    for r in order:
+        peer = (me + r) % 8
+        inner2[r] = go(cut2_ref.at[peer], orb2_ref.at[r], orb2_sem, r, orb_peer(peer))
+    total = mine_ref[rows(ORB_PIECE * me, ORB_PIECE), :]
+    for r in order:
+        spread1[r].wait_recv()
         total = total + orb_ref[r]
     sum_ref[...] = total
     for i in range(16):
-        cut_ref[i] = sum_ref[SLOT * i:SLOT * (i + 1), :]
-    seconds = []
-    for r in range(1, 16):
+        cut_ref[i] = sum_ref[ORB_SLOT * i:ORB_SLOT * (i + 1), :]
+    inner1 = {}
+    for r in sites:
         peer = (here + r) % 16
-        copy = remote(cut_ref.at[peer], site_ref.at[r], site_send.at[r], site_recv.at[r], site_peer(peer))
-        copy.start()
-        seconds.append(copy)
+        inner1[r] = go(cut_ref.at[peer], site_ref.at[r], site_sem, r, site_peer(peer))
+    slot = cut2_ref[me]
+    for r in order:
+        inner2[r].wait_recv()
+        slot = slot + orb2_ref[r]
+    done2_ref[me] = slot
+    outer2 = [
+        go(done2_ref.at[me], done2_ref.at[me], back2_sem, r, orb_peer((me + r) % 8)) for r in order
+    ]
     slot = cut_ref[here]
-    for r, copy in enumerate(seconds, 1):
-        copy.wait_recv()
+    for r in sites:
+        inner1[r].wait_recv()
         slot = slot + site_ref[r]
     done_ref[here] = slot
-    thirds = []
-    for r in range(1, 16):
-        peer = (here + r) % 16
-        copy = remote(done_ref.at[here], done_ref.at[here], back_send.at[r], back_recv.at[r], site_peer(peer))
-        copy.start()
-        thirds.append(copy)
-    for copy in thirds:
+    outer1 = [
+        go(done_ref.at[here], done_ref.at[here], back_sem, r, site_peer((here + r) % 16)) for r in sites
+    ]
+    for copy in outer2:
+        copy.wait_recv()
+    for i in range(8):
+        sum2_ref[SITE_SLOT * i:SITE_SLOT * (i + 1), :] = done2_ref[i]
+    place2 = out_ref.at[rows(SITE_PIECE * here, SITE_PIECE, mine_base + FORTH)]
+    homes2 = [
+        (r, go(sum2_ref, place2, home2_sem, r, site_peer((here + r) % 16))) for r in sites
+    ]
+    lasts = [go(sum2_ref, place2, last2_sem, 0, partner)]
+    out_ref[rows(SITE_PIECE * here, SITE_PIECE, mine_base + FORTH), :] = sum2_ref[...]
+    for copy in outer1:
         copy.wait_recv()
     for i in range(16):
-        sum_ref[SLOT * i:SLOT * (i + 1), :] = done_ref[i]
-    fourths = []
-    for r in order:
-        peer = (me + r) % 8
-        copy = remote(sum_ref, out_ref.at[core, me], home_send.at[r], home_recv.at[r], orb_peer(peer))
-        copy.start()
-        fourths.append(copy)
-    lasts = [remote(sum_ref, out_ref.at[core, me], last_send.at[0], last_recv.at[0], partner)]
-    lasts[0].start()
-    out_ref[core, me] = sum_ref[...]
-    for copy, r in zip(fourths, order):
-        source = (me + 8 - r) % 8
+        sum_ref[ORB_SLOT * i:ORB_SLOT * (i + 1), :] = done_ref[i]
+    place = out_ref.at[rows(ORB_PIECE * me, ORB_PIECE, mine_base)]
+    homes1 = [(r, go(sum_ref, place, home_sem, r, orb_peer((me + r) % 8))) for r in order]
+    lasts.append(go(sum_ref, place, last_sem, 0, partner))
+    out_ref[rows(ORB_PIECE * me, ORB_PIECE, mine_base), :] = sum_ref[...]
+    for r, copy in homes1:
         copy.wait_recv()
-        place = out_ref.at[core, source]
-        forward = remote(place, place, last_send.at[r], last_recv.at[r], partner)
-        forward.start()
-        lasts.append(forward)
+        place = out_ref.at[rows(ORB_PIECE * ((me + 8 - r) % 8), ORB_PIECE, mine_base)]
+        lasts.append(go(place, place, last_sem, r, partner))
+    for r, copy in homes2:
+        copy.wait_recv()
+        place = out_ref.at[rows(SITE_PIECE * ((here + 16 - r) % 16), SITE_PIECE, mine_base + FORTH)]
+        lasts.append(go(place, place, last2_sem, r, partner))
     for copy in lasts:
         copy.wait_recv()
-    return pending + firsts + seconds + thirds + fourths + lasts
+    return every
 
 
 def product(x, y):
@@ -391,7 +449,8 @@
     halo_ref, tile_ref, value_ref, image_ref, top_ref, under_ref, proj24_ref,
     give_ref, take_ref, used_ref, window_ref, dens_ref, ray_all_ref, pot_ref,
     halo_sem, dens_send, dens_recv, give_send, give_recv, used_send, used_recv,
-    top_sem, ray_send, ray_recv, rows_send, rows_recv, sums_send, sums_recv,
+    top_sem, ray_send, ray_recv, sums_send, sums_recv,
+    pad_ref, now_ref, move_ref, rays_ref, early_sem, body_sem, edge_sem, share_sem,
     gram_ref, left_ref, right_ref, *total_scratch,
 ):
     nodes = c_ref.shape[0]
@@ -447,6 +506,8 @@
     density = thrice(split(jnp.broadcast_to(occ_ref[...].reshape(1, 128), (TILE, 128))), split(square), ((1,), (1,)))
     dens_ref[0] = density[0:1, :]
 
+    pad_ref[0:nodes, :] = current
+    pad_ref[nodes:8 * ROWS, :] = jnp.zeros((8 * ROWS - nodes, 128), jnp.float32)
     pl.semaphore_wait(barrier, len(peers))
     halo = remote(
         c_ref.at[pl.ds(0, HALO)], halo_ref, halo_sem.at[0], halo_sem.at[1], cell_peer((here + 31) % 32)
@@ -458,6 +519,29 @@
         copy = remote(dens_ref.at[0], dens_ref.at[r], dens_send.at[r], dens_recv.at[r], orb_peer(peer))
         copy.start()
         dens_copies.append(copy)
+
+    order = (6, 2, 5, 3, 7, 1, 4)
+
+    def edge(index):
+        return pl.ds(pl.multiple_of(EDGE_ROWS * index, 8), EDGE_ROWS)
+
+    def body(index):
+        return pl.ds(pl.multiple_of(8 * EDGE_ROWS + BODY_ROWS * index, 8), BODY_ROWS)
+
+    early = []
+    for r in order:
+        peer = (me + r) % 8
+        for source, target, i in (
+            (body(peer), pl.ds(EDGE_ROWS, BODY_ROWS), 0), (edge(peer), pl.ds(0, EDGE_ROWS), 2)
+        ):
+            copy = remote(
+                pad_ref.at[source], now_ref.at[me, target], early_sem.at[i, r], early_sem.at[i + 1, r],
+                orb_peer(peer),
+            )
+            copy.start()
+            early.append(copy)
+    now_ref[me, 0:EDGE_ROWS, :] = pad_ref[edge(me), :]
+    now_ref[me, EDGE_ROWS:ROWS, :] = pad_ref[body(me), :]
 
     for a in range(DEG):
         for y in range(LINES):
@@ -616,42 +700,71 @@
                 image_ref[start:start + TILE, :] = (
                     image_ref[start:start + TILE, :] + value_ref[s, a, TILE * y:TILE * (y + 1), :]
                 )
+    bodies = []
+    for r in order:
+        peer = (me + r) % 8
+        copy = remote(
+            image_ref.at[body(peer)], move_ref.at[me, pl.ds(EDGE_ROWS, BODY_ROWS)],
+            body_sem.at[0, r], body_sem.at[1, r], orb_peer(peer),
+        )
+        copy.start()
+        bodies.append(copy)
+    move_ref[me, EDGE_ROWS:ROWS, :] = image_ref[body(me), :]
     top.wait_recv()
     image_ref[0:PLANE, :] = image_ref[0:PLANE, :] + under_ref[0:PLANE, :]
+    edges = []
+    for r in order:
+        peer = (me + r) % 8
+        copy = remote(
+            image_ref.at[edge(peer)], move_ref.at[me, pl.ds(0, EDGE_ROWS)],
+            edge_sem.at[0, r], edge_sem.at[1, r], orb_peer(peer),
+        )
+        copy.start()
+        edges.append(copy)
+    move_ref[me, 0:EDGE_ROWS, :] = image_ref[edge(me), :]
     for copy in rays:
         copy.wait_recv()
     total = jnp.sum(ray_all_ref[...], axis=0)
     rayleigh = total[0:1, :] / (total[1:2, :] + tiny)
     ray_ref[...] = rayleigh
-    image_ref[0:nodes, :] = current - step_size * (image_ref[0:nodes, :] - rayleigh * current)
-
-    rows = []
-    for r in (6, 2, 5, 3, 7, 1, 4):
-        peer = (me + r) % 8
-        first = pl.multiple_of(peer * ROWS, TILE)
+    rays_ref[me] = rayleigh
+    shares = []
+    for r in order:
         copy = remote(
-            image_ref.at[pl.ds(first, ROWS)], rows_ref.at[me], rows_send.at[r], rows_recv.at[r],
-            orb_peer(peer),
-        )
-        copy.start()
-        rows.append(copy)
+            rays_ref.at[me], rays_ref.at[me], share_sem.at[0, r], share_sem.at[1, r],
+            orb_peer((me + r) % 8),
+        )
+        copy.start()
+        shares.append(copy)
     sums = []
-    for r in range(1, 32):
+    for r in range(1, 16):
         copy = remote(
             sums_ref.at[here], sums_ref.at[here], sums_send.at[r], sums_recv.at[r],
-            cell_peer((here + r) % 32),
+            site_peer((my_site() + r) % 16),
         )
         copy.start()
         sums.append(copy)
-    rows_ref[me] = image_ref[pl.ds(pl.multiple_of(me * ROWS, TILE), ROWS), :]
-    for copy in rows:
+    for copy in early + shares + bodies + edges:
         copy.wait_recv()
+    for j in range(8):
+        now = now_ref[j]
+        rows_ref[j] = now - step_size * (move_ref[j] - rays_ref[j] * now)
     gram(rows_ref, gram_ref, left_ref, right_ref)
+    core = lax.axis_index("core")
+    passed = []
+    for r in range(16):
+        if r:
+            sums[r - 1].wait_recv()
+        held = sums_ref.at[2 * ((my_site() + 16 - r) % 16) + core]
+        copy = remote(held, held, sums_send.at[16 + r], sums_recv.at[16 + r], {"core": 1 - core})
+        copy.start()
+        passed.append(copy)
     everything = total_over_all(gram_ref, total_ref, *total_scratch)
-    for copy in sums:
+    for copy in passed:
         copy.wait_recv()
+    everything += passed
     everything += [halo, top] + dens_copies + list(gives.values()) + list(useds.values()) + rays
-    for copy in everything + rows + sums:
+    for copy in everything + early + shares + bodies + edges + sums:
         copy.wait_send()
 
 
@@ -668,7 +781,7 @@
     cells = touched_cells.reshape(1, -1) + 10
     hot = jnp.where(jnp.where(line < 10, near, cells) == line, 1.0, 0.0)
     scalars = pl.BlockSpec(memory_space=pltpu.SMEM)
-    dma = lambda n: pltpu.SemaphoreType.DMA((n,))
+    dma = lambda *n: pltpu.SemaphoreType.DMA(n)
     vmem = lambda *shape: pltpu.VMEM(shape, jnp.float32)
     return pl.pallas_call(
         trial_kernel,
@@ -676,7 +789,7 @@
             jax.ShapeDtypeStruct((8, ROWS, 128), jnp.float32),
             jax.ShapeDtypeStruct((1, 128), jnp.float32),
             jax.ShapeDtypeStruct((32, ATOM_DEV, PROJ, 128), jnp.float32),
-            jax.ShapeDtypeStruct((2, 8, PIECE, 128), jnp.float32),
+            jax.ShapeDtypeStruct((36 * 128, 128), jnp.float32),
         ),
         in_specs=[scalars] * 2 + [pl.BlockSpec(memory_space=pltpu.HBM)] * 7,
         out_specs=(WHOLE,) * 4,
@@ -699,14 +812,19 @@
             vmem(32, 2, 128),
             vmem(nodes, 128),
             dma(2), dma(8), dma(8), dma(5), dma(5), dma(5), dma(5),
-            dma(2), dma(32), dma(32), dma(8), dma(8), dma(32), dma(32),
-            vmem(16 * PIECE, 128),
+            dma(2), dma(32), dma(32), dma(32), dma(32),
+            vmem(8 * ROWS, 128), vmem(8, ROWS, 128), vmem(8, ROWS, 128), vmem(8, 1, 128),
+            dma(4, 8), dma(2, 8), dma(2, 8), dma(2, 8),
+            vmem(36 * 128, 128),
             pltpu.VMEM((3 * ROWS, 1024), jnp.bfloat16),
             pltpu.VMEM((3 * ROWS, 1024), jnp.bfloat16),
-            vmem(8, PIECE, 128), vmem(8, PIECE, 128), vmem(8, PIECE, 128), vmem(PIECE, 128),
-            vmem(16, SLOT, 128), vmem(16, SLOT, 128), vmem(16, SLOT, 128),
-            dma(8), dma(8), dma(8), dma(8), dma(16), dma(16),
-            dma(16), dma(16), dma(8), dma(8), dma(8), dma(8),
+            vmem(18 * 128, 128), vmem(18 * 128, 128),
+            vmem(8, ORB_PIECE, 128), vmem(ORB_PIECE, 128), vmem(16, ORB_SLOT, 128),
+            vmem(16, ORB_SLOT, 128), vmem(16, ORB_SLOT, 128),
+            vmem(8, SITE_SLOT, 128), vmem(SITE_PIECE, 128), vmem(8, SITE_SLOT, 128),
+            vmem(16, SITE_PIECE, 128), vmem(8, SITE_SLOT, 128),
+            dma(2, 9), dma(2, 8), dma(2, 16), dma(2, 16), dma(2, 8), dma(2, 8),
+            dma(2, 8), dma(2, 16), dma(2, 8), dma(2, 16), dma(2, 16),
         ],
         compiler_params=pltpu.CompilerParams(
             collective_id=collective_id, has_side_effects=True, vmem_limit_bytes=62 * 1024 * 1024

time: 174 us -> 168 us (0.966)
  Pallas kernels: 168 us -> 162 us
    pallas_call x1, Pallas kernels: 110 us -> 103 us  [trial_rows(): pl.pallas_call(trial_kernel, out_shape=(jax.ShapeDtypeStruct((8, ROWS, 12...]
where the time goes in v4:
time: 168 us; the launch traced here: 167 us
  Pallas kernels  162 us (96%)
  local copies, waits for them, and re-layouts  2.31 us (1%)
  other arithmetic  2.1 us (1%)
    pallas_call x1, Pallas kernels, trial_rows(): pl.pallas_call(trial_kernel, out_shape=(jax.ShapeDtypeStruct((8, ROWS, 12...  103 us
    pallas_call x1, Pallas kernels, solve_rows(): pl.pallas_call(functools.partial(solve_kernel, scale), out_shape=(jax.Sha...  40.7 us
    pallas_call x1, Pallas kernels, rows_back(): pl.pallas_call(rows_back_kernel, out_shape=jax.ShapeDtypeStruct((nodes, 1...  18.7 us

profile of v4, /device:TPU:1, one launch (start us, length us, event | category | flops | bytes accessed | tf_op | source)
XLA Modules:
  0.0 167.5 jit_solution(7925982326883863373)
XLA Ops:
  0.6 0.8 compare_select_fusion.1
  1.4 0.7 add_bitcast_fusion
  2.1 0.7 fusion.hot_ref
  2.7 103.0 %shard_map.130 = (f32[8,272,128]{2,1,0:T(8,128)}, f32[1,128]{1,0:T(1,128)}, f32[32,2,18,128]{3,2,1,0:T(8,128)}, f32[4608,128]{1,0:T(8,128)}) custom-call(f32[9]{0:T(128)} %scale_ref.1, f32[19,6]{1,0:T(8,128)} %fusion.hot_ref, f32[2166,128]{1,0:T(8,128)} %c_in.1, f32[128]{0:T(128)} %occ_in.1, f32[2166]{0:T(1024)} %ext_in.1, f32[2166]{0:T(1024)} %core_in.1, ...), custom_call_target="tpu_custom_call" | custom-call | tf_op jit(solution)/shard_map/pallas_call | solution.py:786
  105.7 40.7 %shard_map.131 = (f32[8,272,128]{2,1,0:T(8,128)}, f32[5,18,128]{2,1,0:T(8,128)}, f32[1,128]{1,0:T(1,128)}) custom-call(s32[64]{0:T(128)} %bitcast.10, f32[36,128,128]{2,1,0:T(8,128)} %bitcast.7, f32[8,272,128]{2,1,0:T(8,128)} %get-tuple-element.11.t_ref, f32[32,2,18,128]{3,2,1,0:T(8,128)} %get-tuple-element.12.sums_ref, f32[1,128]{1,0:T(1,128)} %get-tuple-element.13.ray_ref), custom_call_target="tpu_custom_call" | custom-call | tf_op jit(solution)/shard_map/pallas_call | solution.py:396
  146.4 18.7 %shard_map.132 = f32[2166,128]{1,0:T(8,128)} custom-call(f32[8,272,128]{2,1,0:T(8,128)} %get-tuple-element.14.t_ref), custom_call_target="tpu_custom_call" | custom-call | tf_op jit(solution)/shard_map/pallas_call | solution.py:104
  165.2 2.3 %copy.15 = f32[2166,128]{1,0:T(8,128)} copy(f32[2166,128]{1,0:T(8,128)} %shard_map.132) | data formatting | bytes 2217984
  (1 shorter events, 0.0 us)

commit v5 on v4

--- a/solution.py
+++ b/solution.py
@@ -442,10 +442,10 @@
 
 
 def trial_kernel(
-    scale_ref, hot_ref,
+    scale_ref, atom_ref, cell_ref,
     c_in, occ_in, ext_in, core_in, stiff_in, proj_in, coup_in,
     rows_ref, ray_ref, sums_ref, total_ref,
-    c_ref, occ_ref, ext_ref, core_ref, stiff_ref, proj_ref, coup_ref, pick_ref, load_sem,
+    hot_ref, c_ref, occ_ref, ext_ref, core_ref, stiff_ref, proj_ref, coup_ref, pick_ref, load_sem,
     halo_ref, tile_ref, value_ref, image_ref, top_ref, under_ref, proj24_ref,
     give_ref, take_ref, used_ref, window_ref, dens_ref, ray_all_ref, pot_ref,
     halo_sem, dens_send, dens_recv, give_send, give_recv, used_send, used_recv,
@@ -472,40 +472,9 @@
     ]
     for load in loads:
         load.start()
-    node = lax.broadcasted_iota(jnp.int32, (CELL_NODES, PADDED), 0)
-    place = lax.broadcasted_iota(jnp.int32, (CELL_NODES, PADDED), 1)
-    inside = (place & 7) < EDGE
-    match = node == EDGE * (place >> 3) + (place & 7)
-    spot = jnp.where(inside & match, 1.0, 0.0).astype(jnp.bfloat16)
-    dot = functools.partial(lax.dot_general, preferred_element_type=jnp.float32)
-
-    def both_sides(part):
-        wide = dot(part, spot, (((1,), (0,)), ((), ()))).astype(jnp.bfloat16)
-        return dot(spot, wide, (((0,), (0,)), ((), ()))).astype(jnp.bfloat16)
-
-    loads[0].wait()
-    stiff = tuple(both_sides(part) for part in split(stiff_ref[...]))
-    loads[1].wait()
-    proj24_ref[...] = jnp.zeros_like(proj24_ref)
-    for t in range(TOUCH_DEV):
-        proj24_ref[24 * t:24 * t + PROJ, :] = proj_ref[t, :, 0, :]
-    parts = split(proj24_ref[...])
-    proj_rows = tuple(dot(p, spot, (((1,), (0,)), ((), ()))).astype(jnp.bfloat16) for p in parts)
-    proj_cols = tuple(dot(spot, p, (((0,), (1,)), ((), ()))).astype(jnp.bfloat16) for p in parts)
-
-    loads[2].wait()
-    lane = lax.broadcasted_iota(jnp.int32, (PROJ, 64), 1)
-    for m in range(ATOM_DEV):
-        for p in range(PROJ):
-            column = jnp.sum(jnp.where(lane == 2 * here + m, coup_ref[p], 0.0), axis=1, keepdims=True)
-            pick_ref[m, p] = jnp.broadcast_to(column, (PROJ, 128))
     for load in loads[3:]:
         load.wait()
     current = c_ref[...]
-    square = current * current
-    density = thrice(split(jnp.broadcast_to(occ_ref[...].reshape(1, 128), (TILE, 128))), split(square), ((1,), (1,)))
-    dens_ref[0] = density[0:1, :]
-
     pad_ref[0:nodes, :] = current
     pad_ref[nodes:8 * ROWS, :] = jnp.zeros((8 * ROWS - nodes, 128), jnp.float32)
     pl.semaphore_wait(barrier, len(peers))
@@ -513,6 +482,9 @@
         c_ref.at[pl.ds(0, HALO)], halo_ref, halo_sem.at[0], halo_sem.at[1], cell_peer((here + 31) % 32)
     )
     halo.start()
+    square = current * current
+    density = thrice(split(jnp.broadcast_to(occ_ref[...].reshape(1, 128), (TILE, 128))), split(square), ((1,), (1,)))
+    dens_ref[0] = density[0:1, :]
     dens_copies = []
     for r in range(1, 8):
         peer = (me + r) % 8
@@ -542,6 +514,42 @@
             early.append(copy)
     now_ref[me, 0:EDGE_ROWS, :] = pad_ref[edge(me), :]
     now_ref[me, EDGE_ROWS:ROWS, :] = pad_ref[body(me), :]
+
+    node = lax.broadcasted_iota(jnp.int32, (CELL_NODES, PADDED), 0)
+    place = lax.broadcasted_iota(jnp.int32, (CELL_NODES, PADDED), 1)
+    inside = (place & 7) < EDGE
+    match = node == EDGE * (place >> 3) + (place & 7)
+    spot = jnp.where(inside & match, 1.0, 0.0).astype(jnp.bfloat16)
+    dot = functools.partial(lax.dot_general, preferred_element_type=jnp.float32)
+
+    def both_sides(part):
+        wide = dot(part, spot, (((1,), (0,)), ((), ()))).astype(jnp.bfloat16)
+        return dot(spot, wide, (((0,), (0,)), ((), ()))).astype(jnp.bfloat16)
+
+    loads[0].wait()
+    stiff = tuple(both_sides(part) for part in split(stiff_ref[...]))
+    loads[1].wait()
+    proj24_ref[...] = jnp.zeros_like(proj24_ref)
+    for t in range(TOUCH_DEV):
+        proj24_ref[24 * t:24 * t + PROJ, :] = proj_ref[t, :, 0, :]
+    parts = split(proj24_ref[...])
+    proj_rows = tuple(dot(p, spot, (((1,), (0,)), ((), ()))).astype(jnp.bfloat16) for p in parts)
+    proj_cols = tuple(dot(spot, p, (((0,), (1,)), ((), ()))).astype(jnp.bfloat16) for p in parts)
+
+    loads[2].wait()
+    lane = lax.broadcasted_iota(jnp.int32, (PROJ, 64), 1)
+    for m in range(ATOM_DEV):
+        for p in range(PROJ):
+            column = jnp.sum(jnp.where(lane == 2 * here + m, coup_ref[p], 0.0), axis=1, keepdims=True)
+            pick_ref[m, p] = jnp.broadcast_to(column, (PROJ, 128))
+    for t in range(TOUCH_DEV):
+        for w in range(WINDOW * ATOM_DEV):
+            atom = (2 * (here + w // ATOM_DEV + 32 - REACH) + w % ATOM_DEV) % 64
+            gap = atom_ref[here * TOUCH_DEV + t] - atom
+            hot_ref[w, t] = (1 - jnp.minimum(gap * gap, 1)).astype(jnp.float32)
+        for c in range(SIDE * SIDE):
+            gap = cell_ref[t] - c
+            hot_ref[10 + c, t] = (1 - jnp.minimum(gap * gap, 1)).astype(jnp.float32)
 
     for a in range(DEG):
         for y in range(LINES):
@@ -773,13 +781,6 @@
     touched_atom, touched_cells, projectors, coupling, collective_id,
 ):
     nodes = orbitals.shape[0]
-    here = lax.axis_index(CELLS)
-    mine = lax.dynamic_slice_in_dim(touched_atom, here * TOUCH_DEV, TOUCH_DEV)[None, :]
-    line = lax.broadcasted_iota(jnp.int32, (10 + 9, TOUCH_DEV), 0)
-    near = mine - 2 * here + 2 * REACH
-    near = jnp.where(near < 0, near + 64, jnp.where(near >= 64, near - 64, near))
-    cells = touched_cells.reshape(1, -1) + 10
-    hot = jnp.where(jnp.where(line < 10, near, cells) == line, 1.0, 0.0)
     scalars = pl.BlockSpec(memory_space=pltpu.SMEM)
     dma = lambda *n: pltpu.SemaphoreType.DMA(n)
     vmem = lambda *shape: pltpu.VMEM(shape, jnp.float32)
@@ -791,9 +792,10 @@
             jax.ShapeDtypeStruct((32, ATOM_DEV, PROJ, 128), jnp.float32),
             jax.ShapeDtypeStruct((36 * 128, 128), jnp.float32),
         ),
-        in_specs=[scalars] * 2 + [pl.BlockSpec(memory_space=pltpu.HBM)] * 7,
+        in_specs=[scalars] * 3 + [pl.BlockSpec(memory_space=pltpu.HBM)] * 7,
         out_specs=(WHOLE,) * 4,
         scratch_shapes=[
+            pltpu.SMEM((19, TOUCH_DEV), jnp.float32),
             vmem(nodes, 128), vmem(128), vmem(nodes), vmem(nodes), vmem(CELL_NODES, CELL_NODES),
             vmem(TOUCH_DEV, PROJ, 1, CELL_NODES), vmem(PROJ, PROJ, 64), vmem(ATOM_DEV, PROJ, PROJ, 128),
             dma(7),
@@ -830,7 +832,7 @@
             collective_id=collective_id, has_side_effects=True, vmem_limit_bytes=62 * 1024 * 1024
         ),
     )(
-        cell_scale, hot, orbitals, occupations,
+        cell_scale, touched_atom, touched_cells.reshape(-1), orbitals, occupations,
         external, core_density, stiffness, projectors.transpose(0, 2, 1, 3), coupling.transpose(1, 2, 0),
     )
 

time: 168 us -> 165 us (0.982)
  other arithmetic: 2.1 us -> 0 us
where the time goes in v5:
time: 165 us
  Pallas kernels  162 us (98%)
  local copies, waits for them, and re-layouts  2.31 us (1%)
    pallas_call x1, Pallas kernels, trial_rows(): pl.pallas_call(trial_kernel, out_shape=(jax.ShapeDtypeStruct((8, ROWS, 12...  102 us
    pallas_call x1, Pallas kernels, solve_rows(): pl.pallas_call(functools.partial(solve_kernel, scale), out_shape=(jax.Sha...  40.7 us
    pallas_call x1, Pallas kernels, rows_back(): pl.pallas_call(rows_back_kernel, out_shape=jax.ShapeDtypeStruct((nodes, 1...  18.7 us

profile of v5, /device:TPU:1, one launch (start us, length us, event | category | flops | bytes accessed | tf_op | source)
XLA Modules:
  0.0 164.8 jit_solution(12435705355095720397)
XLA Ops:
  0.6 102.4 %shard_map.130 = (f32[8,272,128]{2,1,0:T(8,128)}, f32[1,128]{1,0:T(1,128)}, f32[32,2,18,128]{3,2,1,0:T(8,128)}, f32[4608,128]{1,0:T(8,128)}) custom-call(f32[9]{0:T(128)} %scale_ref.1, s32[192]{0:T(256)} %atom_ref.1, s32[6]{0:T(128)} %bitcast.9, f32[2166,128]{1,0:T(8,128)} %c_in.1, f32[128]{0:T(128)} %occ_in.1, f32[2166]{0:T(1024)} %ext_in.1, f32[2166]{0:T(1024)} %core_in.1, ...), custom_call_target="tpu_custom_call" | custom-call | tf_op jit(solution)/shard_map/pallas_call | solution.py:787
  103.1 40.7 %shard_map.131 = (f32[8,272,128]{2,1,0:T(8,128)}, f32[5,18,128]{2,1,0:T(8,128)}, f32[1,128]{1,0:T(1,128)}) custom-call(s32[64]{0:T(128)} %bitcast.10, f32[36,128,128]{2,1,0:T(8,128)} %bitcast.6, f32[8,272,128]{2,1,0:T(8,128)} %get-tuple-element.11.t_ref, f32[32,2,18,128]{3,2,1,0:T(8,128)} %get-tuple-element.12.sums_ref, f32[1,128]{1,0:T(1,128)} %get-tuple-element.13.ray_ref), custom_call_target="tpu_custom_call" | custom-call | tf_op jit(solution)/shard_map/pallas_call | solution.py:396
  143.8 18.7 %shard_map.132 = f32[2166,128]{1,0:T(8,128)} custom-call(f32[8,272,128]{2,1,0:T(8,128)} %get-tuple-element.14.t_ref), custom_call_target="tpu_custom_call" | custom-call | tf_op jit(solution)/shard_map/pallas_call | solution.py:104
  162.5 2.3 %copy.15 = f32[2166,128]{1,0:T(8,128)} copy(f32[2166,128]{1,0:T(8,128)} %shard_map.132) | data formatting | bytes 2217984

commit v6 on v5

--- a/solution.py
+++ b/solution.py
@@ -111,7 +111,7 @@
             pltpu.SemaphoreType.DMA((2, 8)), pltpu.SemaphoreType.DMA((2, 8)), pltpu.SemaphoreType.DMA((2,)),
         ],
         compiler_params=pltpu.CompilerParams(
-            collective_id=collective_id, has_side_effects=True, vmem_limit_bytes=58 * 1024 * 1024
+            collective_id=collective_id, has_side_effects=True, vmem_limit_bytes=36 * 1024 * 1024
         ),
     )(value)
 

time: 165 us -> 164 us (level)
  no operation moved by 1% of the time
where the time goes in v6:
time: 164 us
  Pallas kernels  161 us (98%)
  local copies, waits for them, and re-layouts  2.24 us (1%)
    pallas_call x1, Pallas kernels, trial_rows(): pl.pallas_call(trial_kernel, out_shape=(jax.ShapeDtypeStruct((8, ROWS, 12...  102 us
    pallas_call x1, Pallas kernels, solve_rows(): pl.pallas_call(functools.partial(solve_kernel, scale), out_shape=(jax.Sha...  40.7 us
    pallas_call x1, Pallas kernels, rows_back(): pl.pallas_call(rows_back_kernel, out_shape=jax.ShapeDtypeStruct((nodes, 1...  17.5 us

profile of v6, /device:TPU:1, one launch (start us, length us, event | category | flops | bytes accessed | tf_op | source)
XLA Modules:
  0.0 163.5 jit_solution(5065089505589692518)
XLA Ops:
  0.6 102.4 %shard_map.130 = (f32[8,272,128]{2,1,0:T(8,128)}, f32[1,128]{1,0:T(1,128)}, f32[32,2,18,128]{3,2,1,0:T(8,128)}, f32[4608,128]{1,0:T(8,128)}) custom-call(f32[9]{0:T(128)} %scale_ref.1, s32[192]{0:T(256)} %atom_ref.1, s32[6]{0:T(128)} %bitcast.9, f32[2166,128]{1,0:T(8,128)} %c_in.1, f32[128]{0:T(128)} %occ_in.1, f32[2166]{0:T(1024)} %ext_in.1, f32[2166]{0:T(1024)} %core_in.1, ...), custom_call_target="tpu_custom_call" | custom-call | tf_op jit(solution)/shard_map/pallas_call | solution.py:787
  103.1 40.7 %shard_map.131 = (f32[8,272,128]{2,1,0:T(8,128)}, f32[5,18,128]{2,1,0:T(8,128)}, f32[1,128]{1,0:T(1,128)}) custom-call(s32[64]{0:T(128)} %bitcast.10, f32[36,128,128]{2,1,0:T(8,128)} %bitcast.6, f32[8,272,128]{2,1,0:T(8,128)} %get-tuple-element.11.t_ref, f32[32,2,18,128]{3,2,1,0:T(8,128)} %get-tuple-element.12.sums_ref, f32[1,128]{1,0:T(1,128)} %get-tuple-element.13.ray_ref), custom_call_target="tpu_custom_call" | custom-call | tf_op jit(solution)/shard_map/pallas_call | solution.py:396
  143.8 0.0 copy-start
  143.8 1.2 copy-done
  145.0 17.5 %shard_map.132 = f32[2166,128]{1,0:T(8,128)S(1)} custom-call(f32[8,272,128]{2,1,0:T(8,128)S(1)} %copy-done), custom_call_target="tpu_custom_call" | custom-call | tf_op jit(solution)/shard_map/pallas_call | solution.py:104
  162.6 1.0 copy.15
Async XLA Ops:
  143.8 1.2 copy-start
